TPU v7x, 32 devices: a whole 2x2x4 slice. The times are simulated.
32 devices in a mesh: batch: 16 (over z, y, x), stream: 2 (over core).
Axes of the slice: x: 2, y: 2, z: 4, core: 2. Of those that a mesh axis runs over, the one named last changes fastest.
Arguments:
- tokens: bfloat16 [128, 198, 768], P(('batch', 'stream')), may hold values from -6 to 6
- prompts: float32 [50, 768], replicated, may hold values from -6 to 6
- keep_mask: int32 [128, 196], P(('batch', 'stream')), may hold values from 0 to 1, as said below
- counts: int32 [128], P(('batch', 'stream')), may hold values from 79 to 196, as said below
- ln1_gain: float32 [768], replicated, may hold values from 0.5 to 1.5
- ln1_bias: float32 [768], replicated, may hold values from -0.6 to 0.6
- w_qkv: bfloat16 [768, 2304], replicated, may hold values from -0.21875 to 0.21875
- q_bias: float32 [768], replicated, may hold values from -0.6 to 0.6
- v_bias: float32 [768], replicated, may hold values from -0.6 to 0.6
- w_out: bfloat16 [768, 768], replicated, may hold values from -2.5 to 2.5
- out_bias: float32 [768], replicated, may hold values from -0.6 to 0.6
- ln2_gain: float32 [768], replicated, may hold values from 0.5 to 1.5
- ln2_bias: float32 [768], replicated, may hold values from -0.6 to 0.6
- w_fc1: bfloat16 [768, 3072], replicated, may hold values from -0.21875 to 0.21875
- fc1_bias: float32 [3072], replicated, may hold values from -0.6 to 0.6
- w_fc2: bfloat16 [3072, 768], replicated, may hold values from -0.109375 to 0.109375
- fc2_bias: float32 [768], replicated, may hold values from -0.6 to 0.6
- cot_seq: bfloat16 [128, 198, 768], P(('batch', 'stream')), may hold values from -6 to 6
- cot_prompt: bfloat16 [128, 50, 768], P(('batch', 'stream')), may hold values from -6 to 6
Outputs:
- layer_out: bfloat16 [128, 198, 768], P(('batch', 'stream'))
- prompt_out: bfloat16 [128, 50, 768], P(('batch', 'stream'))
- input_grad: float32 [128, 198, 768], P(('batch', 'stream'))
- prompt_grad: float32 [50, 768], replicated
- penalty: float32 [], replicated
Inputs may be any that keep to these rules, and one draw needn't show every extreme that they name: `keep_mask`: 1 keeps a patch; row i has exactly counts[i] ones. counts[i] is the number of ones in row i of keep_mask.
All inputs are finite; a program needn't handle non-finite values.
Results may differ from a plain program's by a relative error of at most 0.01.
Values sent between devices are 32-bit elements; how exact they have to be, the bound alone decides.
A program may use at most 128 MiB of HBM per device.

v0:
```python
import math

import jax
import jax.numpy as jnp
from jax import lax
from jax.sharding import PartitionSpec as P

HEADS = 12


EPSILON = 1e-06


def layer_norm(values_in, norm_gain, norm_shift):
    row_mean = jnp.mean(values_in, axis=-1, keepdims=True)
    centered = values_in - row_mean
    variance = jnp.mean(centered * centered, axis=-1, keepdims=True)
    return centered * lax.rsqrt(variance + EPSILON) * norm_gain + norm_shift


def split_heads(tensor, head_count):
    return tensor.reshape(
        tensor.shape[0], tensor.shape[1], head_count, tensor.shape[2] // head_count
    )


def masked_scores(queries, key_part, live_keys, head_count, score_scale):
    raw_scores = jnp.einsum(
        "iqhd,ikhd->ihqk",
        split_heads(queries, head_count),
        split_heads(key_part, head_count),
        preferred_element_type=jnp.float32,
    )
    return jnp.where(live_keys[:, None, None, :], raw_scores * score_scale, -1e30)


def project_pairs(pair_grads, pair_weight):
    return jnp.einsum("pe,de->pd", pair_grads, pair_weight, precision=lax.Precision.HIGHEST)


def body(
    tokens,
    prompts,
    keep_mask,
    counts,
    ln1_gain,
    ln1_bias,
    w_qkv,
    q_bias,
    v_bias,
    w_out,
    out_bias,
    ln2_gain,
    ln2_bias,
    w_fc1,
    fc1_bias,
    w_fc2,
    fc2_bias,
    cot_seq,
    cot_prompt,
):
    images, seq_length, model_width = tokens.shape
    prompt_count = prompts.shape[0]
    head_count = HEADS
    score_scale = (model_width // head_count) ** (-0.5)
    total_images = images * lax.axis_size("batch") * lax.axis_size("stream")
    count_sum = jnp.sum(counts.astype(jnp.float32))
    kept_total = lax.psum(count_sum, ("batch", "stream"))
    keep_full = jnp.concatenate(
        [jnp.ones((images, seq_length - keep_mask.shape[1]), jnp.int32), keep_mask], axis=1
    )
    kept_cols = keep_full[:, :, None] > 0
    live_keys = (
        jnp.concatenate([jnp.ones((images, prompt_count), jnp.int32), keep_full], axis=1) > 0
    )
    prompt_normed, prompt_norm_back = jax.vjp(
        lambda rows_in: layer_norm(rows_in, ln1_gain, ln1_bias), prompts
    )
    prompt_proj = jnp.dot(
        prompt_normed.astype(jnp.bfloat16), w_qkv, preferred_element_type=jnp.float32
    )
    prompt_query = (prompt_proj[:, :model_width] + q_bias).astype(jnp.bfloat16)
    prompt_pairs = jnp.concatenate(
        [prompt_proj[:, model_width : 2 * model_width], prompt_proj[:, 2 * model_width :] + v_bias],
        axis=1,
    ).astype(jnp.bfloat16)
    token_rows = tokens.astype(jnp.float32)
    token_normed, token_norm_back = jax.vjp(
        lambda rows_in: layer_norm(rows_in, ln1_gain, ln1_bias), token_rows
    )
    token_proj = jnp.einsum(
        "ihd,de->ihe", token_normed.astype(jnp.bfloat16), w_qkv, preferred_element_type=jnp.float32
    )
    token_query = (token_proj[..., :model_width] + q_bias).astype(jnp.bfloat16)
    token_pairs = jnp.concatenate(
        [
            token_proj[..., model_width : 2 * model_width],
            token_proj[..., 2 * model_width :] + v_bias,
        ],
        axis=2,
    ).astype(jnp.bfloat16)
    queries = jnp.concatenate(
        [jnp.broadcast_to(prompt_query[None], (images, prompt_count, model_width)), token_query],
        axis=1,
    )
    pairs = jnp.concatenate(
        [
            jnp.broadcast_to(prompt_pairs[None], (images, prompt_count, 2 * model_width)),
            token_pairs,
        ],
        axis=1,
    )
    key_part = pairs[..., :model_width]
    value_part = pairs[..., model_width:]
    value_heads = split_heads(value_part, head_count)
    scores = masked_scores(queries, key_part, live_keys, head_count, score_scale)
    top_score = jnp.max(scores, axis=-1, keepdims=True)
    log_total = top_score + jnp.log(jnp.sum(jnp.exp(scores - top_score), axis=-1, keepdims=True))
    soft_low = jnp.exp(scores - log_total).astype(jnp.bfloat16)
    context = jnp.einsum(
        "ihqk,ikhd->iqhd", soft_low, value_heads, preferred_element_type=jnp.float32
    )
    context = context.reshape(images, -1, model_width).astype(jnp.bfloat16)
    attention = (
        jnp.einsum("ird,de->ire", context, w_out, preferred_element_type=jnp.float32) + out_bias
    )
    residual = jnp.concatenate(
        [jnp.broadcast_to(prompts[None], (images, prompt_count, model_width)), token_rows], axis=1
    )
    middle = residual + attention
    second_norm, second_norm_back = jax.vjp(
        lambda rows_in: layer_norm(rows_in, ln2_gain, ln2_bias), middle
    )
    hidden = (
        jnp.einsum(
            "ird,df->irf",
            second_norm.astype(jnp.bfloat16),
            w_fc1,
            preferred_element_type=jnp.float32,
        )
        + fc1_bias
    )
    activated, gelu_back = jax.vjp(lambda rows_in: jax.nn.gelu(rows_in, approximate=False), hidden)
    result = (
        middle
        + jnp.einsum(
            "irf,fd->ird", activated.astype(jnp.bfloat16), w_fc2, preferred_element_type=jnp.float32
        )
        + fc2_bias
    )
    prompt_out = result[:, :prompt_count].astype(jnp.bfloat16)
    layer_out = jnp.where(kept_cols, result[:, prompt_count:], token_rows).astype(jnp.bfloat16)
    grad_result = jnp.concatenate(
        [cot_prompt, jnp.where(kept_cols, cot_seq, jnp.zeros_like(cot_seq))], axis=1
    )
    grad_act = jnp.einsum("ird,fd->irf", grad_result, w_fc2, preferred_element_type=jnp.float32)
    grad_hidden = gelu_back(grad_act)[0].astype(jnp.bfloat16)
    grad_second = jnp.einsum("irf,df->ird", grad_hidden, w_fc1, preferred_element_type=jnp.float32)
    grad_middle = grad_result.astype(jnp.float32) + second_norm_back(grad_second)[0]
    grad_context = jnp.einsum(
        "ire,de->ird", grad_middle.astype(jnp.bfloat16), w_out, preferred_element_type=jnp.float32
    ).astype(jnp.bfloat16)
    again = masked_scores(queries, key_part, live_keys, head_count, score_scale)
    soft_full = jnp.exp(again - log_total)
    soft_back = soft_full.astype(jnp.bfloat16)
    context_heads = split_heads(grad_context, head_count)
    grad_soft = jnp.einsum(
        "iqhd,ikhd->ihqk", context_heads, value_heads, preferred_element_type=jnp.float32
    )
    grad_values = jnp.einsum(
        "ihqk,iqhd->ikhd", soft_back, context_heads, preferred_element_type=jnp.float32
    ).reshape(images, -1, model_width)
    row_dot = jnp.sum(soft_full * grad_soft, axis=-1, keepdims=True)
    grad_scores = (soft_full * (grad_soft - row_dot)).astype(jnp.bfloat16)
    grad_queries = (
        jnp.einsum(
            "ihqk,ikhd->iqhd",
            grad_scores,
            split_heads(key_part, head_count),
            preferred_element_type=jnp.float32,
        )
        * score_scale
    )
    grad_queries = grad_queries.reshape(images, -1, model_width).astype(jnp.bfloat16)
    grad_keys = (
        jnp.einsum(
            "ihqk,iqhd->ikhd",
            grad_scores,
            split_heads(queries, head_count),
            preferred_element_type=jnp.float32,
        )
        * score_scale
    ).reshape(images, -1, model_width)
    grad_pairs = jnp.concatenate([grad_keys, grad_values], axis=2)
    token_proj_grad = jnp.concatenate(
        [grad_queries[:, prompt_count:], grad_pairs[:, prompt_count:].astype(jnp.bfloat16)], axis=2
    )
    grad_token_normed = jnp.einsum(
        "ihe,de->ihd", token_proj_grad, w_qkv, preferred_element_type=jnp.float32
    )
    grad_tokens = grad_middle[:, prompt_count:] + token_norm_back(grad_token_normed)[0]
    input_grad = jnp.where(kept_cols, grad_tokens, cot_seq.astype(jnp.float32))
    pair_weight = w_qkv[:, model_width:].astype(jnp.float32)
    pair_local = jnp.sum(grad_pairs[:, :prompt_count], axis=0)
    query_normed = jnp.sum(
        jnp.einsum(
            "ipe,de->ipd",
            grad_queries[:, :prompt_count],
            w_qkv[:, :model_width],
            preferred_element_type=jnp.float32,
        ),
        axis=0,
    )
    middle_sum = jnp.sum(grad_middle[:, :prompt_count], axis=0)
    prompt_local = prompt_norm_back(query_normed)[0] + middle_sum
    pair_total = lax.psum(pair_local, ("batch", "stream"))
    prompt_total = lax.psum(prompt_local, ("batch", "stream"))
    prompt_total = prompt_total + prompt_norm_back(project_pairs(pair_total, pair_weight))[0]
    penalty_weight = kept_total / (keep_mask.shape[1] * math.sqrt(total_images))
    prompt_grad = prompt_total + 2.0 * penalty_weight * prompts
    penalty = penalty_weight * jnp.sum(prompts * prompts) / (prompt_count * model_width)
    return (layer_out, prompt_out, input_grad, prompt_grad, penalty)


def solution(mesh):
    in_specs = (
        P(("batch", "stream"), None, None),
        P(),
        P(("batch", "stream"), None),
        P(("batch", "stream")),
        P(),
        P(),
        P(),
        P(),
        P(),
        P(),
        P(),
        P(),
        P(),
        P(),
        P(),
        P(),
        P(),
        P(("batch", "stream"), None, None),
        P(("batch", "stream"), None, None),
    )
    out_specs = (
        P(("batch", "stream"), None, None),
        P(("batch", "stream"), None, None),
        P(("batch", "stream"), None, None),
        P(),
        P(),
    )
    return jax.shard_map(body, mesh=mesh, in_specs=in_specs, out_specs=out_specs, check_vma=False)
```

profile of v0, /device:TPU:0, one launch (start us, length us, event | category | flops | bytes accessed | tf_op | source)
XLA Modules:
  0.0 463.0 jit_solution(8597299555711745016)
XLA Ops:
  10.7 5.8 %fusion.29 = f32[4,198,2304]{2,1,0:T(8,128)S(1)} fusion(bf16[768,2304]{1,0:T(8,128)(2,1)} %param.25, f32[768]{0:T(1024)} %param.24, f32[768]{0:T(1024)} %param.23, f32[4,198]{1,0:T(4,128)S(1)} %fusion.73, f32[4,198]{1,0:T(4,128)S(1)} %broadcast_multiply_fusion.1, bf16[4,198,768]{2,0,1:T(4,128)(2,1)} %param.19), kind=kOutput, calls=%fused_computation.49 | convolution fusion | flops 2806493184 | bytes 12067008 | tf_op jit(solution)/shard_map/ihd,de->ihe/dot_general | solution.py:91
  16.5 3.0 copy-done.17
  23.8 4.0 fusion.35
  42.9 5.0 %fusion.6 = (f32[4,12,248]{2,1,0:T(8,128)S(1)}, f32[4,12,248,248]{2,3,1,0:T(8,128)S(1)}) fusion(pred[4,248]{1,0:T(4,128)(4,1)S(1)} %add_compare_fusion, bf16[4,248,12,64]{1,3,2,0:T(8,128)(2,1)} %bitcast.72, bf16[4,248,12,64]{1,3,2,0:T(8,128)(2,1)} %bitcast.70), kind=kOutput, calls=%fused_computation.26 | convolution fusion | flops 386725248 | bytes 14904800 | tf_op jit(solution)/shard_map/iqhd,ikhd->ihqk/dot_general | solution.py:28
  47.9 3.4 exponential_reduce_fusion
  52.5 3.1 convolution_convert_fusion
  58.8 13.1 %fusion.32 = (u8[248,3072]{1,0:T(8,128)(4,1)S(1)}, u8[248,3072]{1,0:T(8,128)(4,1)S(1)}, f32[4,248,3072]{2,1,0:T(8,128)}) fusion(f32[3072]{0:T(1024)S(1)} %copy-done.29, bf16[768,3072]{1,0:T(8,128)(2,1)S(1)} %bitcast.83, f32[4,248,768]{2,1,0:T(8,128)S(1)} %get-tuple-element.36, f32[768]{0:T(1024)S(1)} %copy-done.34, f32[768]{0:T(1024)S(1)} %copy-done.25, ...), kind=kOutput, calls=%fused_computation.60 | convolution fusion | flops 4725792768 | bytes 21505792 | tf_op jit(solution)/shard_map/ird,df->irf/dot_general | solution.py:135
  71.9 29.0 %fusion = f32[4,248,3072]{2,1,0:T(8,128)} fusion(f32[4,248,3072]{2,1,0:T(8,128)} %get-tuple-element.37, f32[3072]{0:T(1024)S(1)} %copy-done.29, u8[248,3072]{1,0:T(8,128)(4,1)S(1)} %get-tuple-element.16, u8[248,3072]{1,0:T(8,128)(4,1)S(1)} %get-tuple-element.15), kind=kLoop, calls=%fused_computation.1 | loop fusion | flops 207224832 | bytes 25915392 | tf_op jit(solution)/shard_map/jvp()/erfc | solution.py:143
  100.9 14.7 %add_add_fusion.3 = bf16[4,248,768]{2,1,0:T(8,128)(2,1)S(1)} fusion(f32[4,248,768]{2,1,0:T(8,128)S(1)} %get-tuple-element.36, bf16[3072,768]{1,0:T(8,128)(2,1)} %param.34, f32[4,248,3072]{2,1,0:T(8,128)} %fusion, f32[4,248,3072]{2,1,0:T(8,128)} %get-tuple-element.37, f32[3072]{0:T(1024)S(1)} %copy-done.29, f32[768]{0:T(1024)S(1)} %copy-done.35), kind=kOutput, calls=%fused_computation.56 | convolution fusion | flops 4695318528 | bytes 33684480 | tf_op jit(solution)/shard_map/irf,fd->ird/dot_general | solution.py:146
  117.9 19.5 %multiply_reduce_fusion.1 = (f32[4,248]{1,0:T(4,128)S(1)}, f32[4,248,768]{2,1,0:T(8,128)}) fusion(f32[4,248,768]{2,1,0:T(8,128)} %copy-done.4, f32[768]{0:T(1024)S(1)} %copy-done.25, f32[4,248]{1,0:T(4,128)S(1)} %broadcast_multiply_fusion, bf16[768,3072]{1,0:T(8,128)(2,1)} %param.32, f32[4,248,3072]{2,1,0:T(8,128)} %fusion, ...), kind=kOutput, calls=%fused_computation.55 | convolution fusion | flops 9413491712 | bytes 41458432 | tf_op jit(solution)/shard_map/irf,df->ird/dot_general | solution.py:158
  137.5 3.5 fusion.60
  151.5 14.3 %multiply_reduce_fusion = (f32[4,12,248]{2,1,0:T(8,128)S(1)}, f32[4,12,248,248]{2,3,1,0:T(8,128)}) fusion(f32[4,12,248,248]{2,3,1,0:T(8,128)} %copy-done.1, f32[4,12,248]{2,1,0:T(8,128)S(1)} %log_add_fusion, pred[4,248]{1,0:T(4,128)(4,1)S(1)} %add_compare_fusion, bf16[4,248,12,64]{1,3,2,0:T(8,128)(2,1)} %bitcast.74, bf16[4,248,12,64]{1,3,2,0:T(8,128)(2,1)} %bitcast.80), kind=kOutput, calls=%fused_computation.8 | convolution fusion | flops 392629632 | bytes 26761184 | tf_op jit(solution)/shard_map/iqhd,ikhd->ihqk/dot_general | solution.py:167
  165.8 9.0 %fusion.64 = f32[4,12,64,248]{3,2,1,0:T(8,128)} fusion(bf16[4,248,12,64]{1,3,2,0:T(8,128)(2,1)S(1)} %bitcast.75, f32[4,12,248,248]{2,3,1,0:T(8,128)} %copy-done.1, f32[4,12,248]{2,1,0:T(8,128)S(1)} %log_add_fusion, pred[4,248]{1,0:T(4,128)(4,1)S(1)} %add_compare_fusion), kind=kOutput, calls=%fused_computation.121 | convolution fusion | flops 389689344 | bytes 16428512 | tf_op jit(solution)/shard_map/ihqk,iqhd->ikhd/dot_general | solution.py:170
  174.8 6.9 %multiply_convert_fusion = bf16[4,12,248,248]{2,3,1,0:T(8,128)(2,1)S(1)} fusion(f32[4,12,248,248]{2,3,1,0:T(8,128)} %get-tuple-element.41, f32[4,12,248,248]{2,3,1,0:T(8,128)S(1)} %bitcast.69, f32[4,12,248]{2,1,0:T(8,128)S(1)} %get-tuple-element.40, f32[4,12,248]{2,1,0:T(8,128)S(1)} %log_add_fusion, pred[4,248]{1,0:T(4,128)(4,1)S(1)} %add_compare_fusion), kind=kLoop, calls=%fused_computation.7 | loop fusion | flops 17713152 | bytes 29618144 | tf_op jit(solution)/shard_map/convert_element_type | solution.py:174
  181.8 3.7 convolution_multiply_fusion
  185.5 3.5 copy.61
  189.0 3.6 copy.62
  195.1 4.5 fusion.13
  199.6 3.9 multiply_convert_fusion.3
  209.0 6.3 %multiply_reduce_fusion.3 = (f32[4,198]{1,0:T(4,128)S(1)}, f32[4,198,768]{2,1,0:T(8,128)S(1)}) fusion(f32[768]{0:T(1024)S(1)} %copy-done.24, f32[4,198]{1,0:T(4,128)S(1)} %broadcast_multiply_fusion.1, bf16[4,198,768]{2,0,1:T(4,128)(2,1)S(1)} %copy-done.3, bf16[768,2304]{1,0:T(8,128)(2,1)} %param.25, bf16[4,198,1536]{2,1,0:T(8,128)(2,1)} %fusion.13, ...), kind=kOutput, calls=%fused_computation.70 | convolution fusion | flops 2813183232 | bytes 10847424 | tf_op jit(solution)/shard_map/ihe,de->ihd/dot_general | solution.py:198
  222.3 42.2 %psum.23 = f32[]{:T(128)} all-reduce(f32[]{:T(128)} %convert_reduce_fusion.1), channel_id=1, replica_groups=mesh['batch'=16,'stream'=2] {'batch','stream'}, use_global_device_ids=true, to_apply=%region_23.24 | all-reduce | flops 1 | bytes 8 | tf_op jit(solution)/shard_map/psum | solution.py:68
  273.2 50.1 %all-reduce.6.cloned.1.call-done = f32[50,1536]{1,0:T(8,128)} async-done(((f32[50,1536]{1,0:T(8,128)}), f32[50,1536]{1,0:T(8,128)}) %all-reduce.6.cloned.1.call-update) | async-done | bytes 307216 | tf_op jit(solution)/shard_map/psum | solution.py:216
  323.3 4.6 multiply_reduce_fusion.5
  329.8 123.3 %all-reduce.4.cloned.1.call-done = f32[50,768]{1,0:T(8,128)} async-done(((f32[50,768]{1,0:T(8,128)}), f32[50,768]{1,0:T(8,128)}) %all-reduce.4.cloned.1.call-update) | async-done | bytes 153616 | tf_op jit(solution)/shard_map/psum | solution.py:217
  (152 shorter events, 64.9 us)
Async XLA Ops:
  7.2 48.5 %copy-start = (bf16[768,768]{1,0:T(8,128)(2,1)S(1)}, bf16[768,768]{1,0:T(8,128)(2,1)}, u32[]{:S(2)}) copy-start(bf16[768,768]{1,0:T(8,128)(2,1)} %param.28) | copy-start | bytes 3538948
  7.2 316.1 %all-reduce.6.cloned.1.call-start = ((), (), s32[]{:S(2)}) async-start(), calls=%async_computation.1 | async-start | bytes 688128 | tf_op jit(solution)/shard_map/psum | solution.py:216
  10.6 10.0 %copy-start.12 = (f32[50,768]{1,0:T(8,128)S(1)}, f32[50,768]{1,0:T(8,128)}, u32[]{:S(2)}) copy-start(f32[50,768]{1,0:T(8,128)} %param.20) | copy-start | bytes 460804
  10.6 10.3 %copy-start.24 = (f32[768]{0:T(1024)S(1)}, f32[768]{0:T(1024)}, u32[]{:S(2)}) copy-start(f32[768]{0:T(1024)} %param.23) | copy-start | bytes 9220
  10.7 10.3 %copy-start.30 = (f32[768]{0:T(1024)S(1)}, f32[768]{0:T(1024)}, u32[]{:S(2)}) copy-start(f32[768]{0:T(1024)} %param.24) | copy-start | bytes 9220
  19.5 4.3 copy-start.26
  19.5 4.3 copy-start.27
  23.8 4.1 copy-start.3
  47.9 4.6 copy-start.1
  47.9 4.6 copy-start.16
  57.5 43.4 %copy-start.4 = (f32[4,248,768]{2,1,0:T(8,128)}, f32[4,248,768]{2,1,0:T(8,128)S(1)}, u32[]{:S(2)}) copy-start(f32[4,248,768]{2,1,0:T(8,128)S(1)} %get-tuple-element.36) | copy-start | bytes 9142276
  71.9 29.0 %copy-start.35 = (f32[768]{0:T(1024)S(1)}, f32[768]{0:T(1024)}, u32[]{:S(2)}) copy-start(f32[768]{0:T(1024)} %param.35) | copy-start | bytes 9220
  100.9 14.7 %copy-start.19 = (bf16[4,198,768]{2,0,1:T(4,128)(2,1)S(1)}, bf16[4,198,768]{2,0,1:T(4,128)(2,1)}, u32[]{:S(2)}) copy-start(bf16[4,198,768]{2,0,1:T(4,128)(2,1)} %param.36) | copy-start | bytes 3649540
  137.5 4.6 copy-start.11
  151.5 14.4 %copy-start.8 = (bf16[4,248,768]{1,2,0:T(8,128)(2,1)S(1)}, bf16[4,248,768]{1,2,0:T(8,128)(2,1)}, u32[]{:S(2)}) copy-start(bf16[4,248,768]{1,2,0:T(8,128)(2,1)} %copy.56) | copy-start | bytes 4571140
  151.5 23.4 %slice-start = ((s8[12189696]{0:T(1024)(128)(4,1)}), s8[4194304]{0:T(1024)(128)(4,1)S(1)}, s32[]{:S(2)}) async-start(s8[12189696]{0:T(1024)(128)(4,1)} %bitcast.68), calls=%async_computation.2 | async-start | bytes 8388608
  151.5 23.4 %slice-start.1 = ((s8[12189696]{0:T(1024)(128)(4,1)}), s8[3801088]{0:T(1024)(128)(4,1)S(1)}, s32[]{:S(2)}) async-start(s8[12189696]{0:T(1024)(128)(4,1)} %bitcast.68), calls=%async_computation.3 | async-start | bytes 7602176
  165.8 9.0 %slice-start.2 = ((s8[12189696]{0:T(1024)(128)(4,1)}), s8[4194304]{0:T(1024)(128)(4,1)S(1)}, s32[]{:S(2)}) async-start(s8[12189696]{0:T(1024)(128)(4,1)} %bitcast.68), calls=%async_computation.4 | async-start | bytes 8388608
  174.8 7.0 %copy-start.7 = (bf16[4,248,768]{1,2,0:T(8,128)(2,1)S(1)}, bf16[4,248,768]{1,2,0:T(8,128)(2,1)}, u32[]{:S(2)}) copy-start(bf16[4,248,768]{1,2,0:T(8,128)(2,1)} %copy.50) | copy-start | bytes 4571140
  194.8 258.3 %all-reduce.4.cloned.1.call-start = ((), (), s32[]{:S(2)}) async-start(), calls=%async_computation | async-start | bytes 344064 | tf_op jit(solution)/shard_map/psum | solution.py:217
  195.1 4.6 copy-start.6
  209.0 7.3 %copy-start.20 = (bf16[4,198,768]{2,0,1:T(4,128)(2,1)S(1)}, bf16[4,198,768]{2,0,1:T(4,128)(2,1)}, u32[]{:S(2)}) copy-start(bf16[4,198,768]{2,0,1:T(4,128)(2,1)} %param.36) | copy-start | bytes 3649540
  220.2 47.3 %slice-start.3 = ((bf16[4,248,768]{2,1,0:T(8,128)(2,1)}), bf16[4,50,768]{2,1,0:T(8,128)(2,1)S(1)}, s32[]{:S(2)}) async-start(bf16[4,248,768]{2,1,0:T(8,128)(2,1)} %copy-done.22), calls=%async_computation.5 | async-start | bytes 688128 | tf_op jit(solution)/shard_map/slice | solution.py:151
  270.7 57.2 %copy-start.32 = (f32[50]{0:T(128)S(1)}, f32[50]{0:T(128)}, u32[]{:S(2)}) copy-start(f32[50]{0:T(128)} %copy-done.31) | copy-start | bytes 604
  (21 other events, 50.5 us)
Sparse Core Ops, SparseCore 0:
  194.9 128.3 all-reduce.5
  330.3 122.7 all-reduce.3
where the time goes:
time: 470 us; the launch traced here: 463 us
  waiting for transfers between devices  173 us (37%)
  matrix products  112 us (24%)
  other arithmetic  75.7 us (16%)
  blocking collectives  42.2 us (9%)
  local copies, waits for them, and re-layouts  41.1 us (9%)
  between operations  17.9 us (4%)
    psum x1, waiting for transfers between devices, body(): prompt_total = lax.psum(prompt_local, ('batch', 'stream'))  123 us
    psum x1, waiting for transfers between devices, body(): pair_total = lax.psum(pair_local, ('batch', 'stream'))  50.1 us
    psum x1, blocking collectives, body(): kept_total = lax.psum(count_sum, ('batch', 'stream'))  42.2 us
    another operation x1, other arithmetic, body(): jax.nn.gelu(rows_in, approximate=False)  29 us
    dot_general x1, matrix products, body(): jnp.einsum('irf,df->ird', grad_hidden, w_fc1, preferred_element_type=jnp....  19.5 us
    unnamed x89, local copies, waits for them, and re-layouts  18.5 us
    dot_general x1, matrix products, body(): jnp.einsum('irf,fd->ird', activated.astype(jnp.bfloat16), w_fc2, preferre...  14.7 us
    dot_general x1, matrix products, body(): jnp.einsum('iqhd,ikhd->ihqk', context_heads, value_heads, preferred_eleme...  14.3 us
  transfers between devices with their start and end apart: 2, of which 2 were waited for; matrix products, arithmetic and copies ran while one was open for 7% of the time, Pallas kernels for 0%

commit v1 on v0

v1 whole, which is shorter than its diff:
```python
import functools
import math

import jax
import jax.numpy as jnp
from jax import lax
from jax.experimental import pallas as pl
from jax.experimental.pallas import tpu as pltpu
from jax.sharding import PartitionSpec as P

HEADS = 12
EPSILON = 1e-06
F32 = jnp.float32
BF16 = jnp.bfloat16
MESH = pl.DeviceIdType.MESH
DEAD = -1e30

NN = (((1,), (0,)), ((), ()))
NT = (((1,), (1,)), ((), ()))


def dot(a, b, dims=NN):
    return lax.dot_general(a, b, dims, preferred_element_type=F32)


def round_up(value, step):
    return -(-value // step) * step


def norm_stats(rows_in):
    mean = jnp.mean(rows_in, axis=-1, keepdims=True)
    centered = rows_in - mean
    variance = jnp.mean(centered * centered, axis=-1, keepdims=True)
    scale = lax.rsqrt(variance + EPSILON)
    return centered * scale, scale


def norm_back(grad, gain, unit, scale):
    scaled = grad * gain
    mean = jnp.mean(scaled, axis=-1, keepdims=True)
    along = jnp.mean(scaled * unit, axis=-1, keepdims=True)
    return scale * (scaled - mean - unit * along)


def layer_kernel(
    tokens_ref,
    prompts_ref,
    keep_ref,
    counts_ref,
    ln1_gain_ref,
    ln1_bias_ref,
    q_bias_ref,
    v_bias_ref,
    out_bias_ref,
    ln2_gain_ref,
    ln2_bias_ref,
    fc1_bias_ref,
    fc2_bias_ref,
    cot_seq_ref,
    cot_prompt_ref,
    w_qkv_hbm,
    w_out_hbm,
    w_fc1_hbm,
    w_fc2_hbm,
    layer_out_ref,
    prompt_out_ref,
    input_grad_ref,
    prompt_local_ref,
    w_qkv,
    w_out,
    w_fc1,
    w_fc2,
    rows_s,
    cot_s,
    normed_s,
    q_s,
    k_s,
    v_s,
    kt_s,
    vt_s,
    qm_s,
    gm_s,
    soft_s,
    ctx_s,
    act_s,
    gh_s,
    mid_s,
    gmid_s,
    dqkv_s,
    sum_s,
    gmid_sum_s,
    sems,
):
    image = pl.program_id(0)
    images = pl.num_programs(0)
    seq, width = tokens_ref.shape[1], tokens_ref.shape[2]
    prompt_count = prompts_ref.shape[0]
    patches = keep_ref.shape[1]
    lead = seq - patches
    head_dim = width // HEADS
    hidden = w_fc1.shape[1]
    total = rows_s.shape[0]
    first = round_up(seq, 8)
    score_scale = head_dim ** (-0.5)
    step_rows = 64

    copies = [
        pltpu.make_async_copy(src, dst, sems.at[at])
        for at, (src, dst) in enumerate(
            ((w_qkv_hbm, w_qkv), (w_out_hbm, w_out), (w_fc1_hbm, w_fc1), (w_fc2_hbm, w_fc2))
        )
    ]

    @pl.when(image == 0)
    def _():
        for copy in copies:
            copy.start()
        rows_s[...] = jnp.zeros_like(rows_s)
        cot_s[...] = jnp.zeros_like(cot_s)
        sum_s[...] = jnp.zeros_like(sum_s)
        gmid_sum_s[...] = jnp.zeros_like(gmid_sum_s)
        rows_s[first : first + prompt_count, :] = prompts_ref[...]

    at_row = lax.broadcasted_iota(jnp.int32, (total, patches), 0)
    at_col = lax.broadcasted_iota(jnp.int32, (total, patches), 1)
    keep_row = keep_ref[pl.ds(image, 1), :].astype(F32)
    patch_kept = jnp.sum(
        jnp.where(at_row == at_col + lead, keep_row, 0.0), axis=1, keepdims=True
    )
    row_at = lax.broadcasted_iota(jnp.int32, (total, 1), 0)
    is_prompt = (row_at >= first) & (row_at < first + prompt_count)
    live = (row_at < lead) | is_prompt | (patch_kept > 0.0)
    dead_add = jnp.where(live, 0.0, DEAD)
    token_kept = live[:seq]

    rows_s[:seq, :] = tokens_ref[0].astype(F32)
    cot_s[:seq, :] = jnp.where(token_kept, cot_seq_ref[0].astype(F32), 0.0)
    cot_s[first : first + prompt_count, :] = cot_prompt_ref[0].astype(F32)

    gain1 = ln1_gain_ref[...]
    bias1 = ln1_bias_ref[...]
    for at in range(0, total, step_rows):
        unit, _ = norm_stats(rows_s[at : at + step_rows, :])
        normed_s[at : at + step_rows, :] = (unit * gain1 + bias1).astype(BF16)

    @pl.when(image == 0)
    def _():
        copies[0].wait()

    normed = normed_s[...]
    q_s[...] = (
        (dot(normed, w_qkv[:, :width]) + q_bias_ref[...]).astype(BF16) * jnp.asarray(score_scale, BF16)
    )
    k_s[...] = dot(normed, w_qkv[:, width : 2 * width]).astype(BF16)
    v_s[...] = (dot(normed, w_qkv[:, 2 * width :]) + v_bias_ref[...]).astype(BF16)
    kt_s[...] = k_s[...].T
    vt_s[...] = v_s[...].T

    lane = lax.broadcasted_iota(jnp.int32, (total, 2 * head_dim), 1)
    low_half = lane < head_dim
    for pair in range(HEADS // 2):
        cols = slice(pair * 2 * head_dim, (pair + 1) * 2 * head_dim)
        q_pair = q_s[:, cols]
        for half in range(2):
            head = 2 * pair + half
            picked = low_half if half == 0 else ~low_half
            qm = jnp.where(picked, q_pair, jnp.zeros_like(q_pair))
            qm_s[head] = qm
            scores = dot(k_s[:, cols], qm, NT) + dead_add
            top = jnp.max(scores, axis=0, keepdims=True)
            weight = jnp.exp(scores - top)
            soft = weight * (1.0 / jnp.sum(weight, axis=0, keepdims=True))
            soft_low = soft.astype(BF16)
            soft_s[head] = soft_low
            ctx_s[head * head_dim : (head + 1) * head_dim, :] = dot(
                vt_s[head * head_dim : (head + 1) * head_dim, :], soft_low
            ).astype(BF16)

    @pl.when(image == 0)
    def _():
        copies[1].wait()

    context = ctx_s[...].T
    mid_s[...] = dot(context, w_out[...]) + out_bias_ref[...] + rows_s[...]
    gain2 = ln2_gain_ref[...]
    bias2 = ln2_bias_ref[...]
    for at in range(0, total, step_rows):
        unit, _ = norm_stats(mid_s[at : at + step_rows, :])
        normed_s[at : at + step_rows, :] = (unit * gain2 + bias2).astype(BF16)

    @pl.when(image == 0)
    def _():
        copies[2].wait()
        copies[3].wait()

    second = normed_s[...]
    grad_result = cot_s[...].astype(BF16)
    chunk = 2 * 128
    for at in range(0, hidden, chunk):
        cols = slice(at, at + chunk)
        pre = dot(second, w_fc1[:, cols]) + fc1_bias_ref[:, cols]
        share = 0.5 + 0.5 * lax.erf(pre * (0.5**0.5))
        density = jnp.exp(pre * pre * -0.5) * ((2.0 * math.pi) ** -0.5)
        act_s[:, cols] = (pre * share).astype(BF16)
        grad_act = dot(grad_result, w_fc2[cols, :], NT)
        gh_s[:, cols] = (grad_act * (share + pre * density)).astype(BF16)

    result = dot(act_s[...], w_fc2[...]) + fc2_bias_ref[...] + mid_s[...]
    layer_out_ref[0] = jnp.where(token_kept, result[:seq], rows_s[:seq, :]).astype(BF16)
    prompt_out_ref[0] = result[first : first + prompt_count].astype(BF16)

    gmid_s[...] = dot(gh_s[...], w_fc1[...], NT)
    for at in range(0, total, step_rows):
        part = slice(at, at + step_rows)
        unit, scale = norm_stats(mid_s[part, :])
        gmid = cot_s[part, :] + norm_back(gmid_s[part, :], gain2, unit, scale)
        gmid_s[part, :] = gmid
        normed_s[part, :] = gmid.astype(BF16)
    gctx = dot(normed_s[...], w_out[...], NT).astype(BF16)

    for pair in range(HEADS // 2):
        cols = slice(pair * 2 * head_dim, (pair + 1) * 2 * head_dim)
        key_grad = None
        value_grad = None
        for half in range(2):
            head = 2 * pair + half
            picked = low_half if half == 0 else ~low_half
            gctx_pair = gctx[:, cols]
            gm = jnp.where(picked, gctx_pair, jnp.zeros_like(gctx_pair))
            soft_low = soft_s[head]
            soft = soft_low.astype(F32)
            grad_soft = soft * dot(v_s[:, cols], gm, NT)
            row_dot = jnp.sum(grad_soft, axis=0, keepdims=True)
            grad_scores = (grad_soft - soft * row_dot).astype(BF16)
            gv = dot(soft_low, gm)
            gk = dot(grad_scores, qm_s[head])
            value_grad = gv if half == 0 else value_grad + gv
            key_grad = gk if half == 0 else key_grad + gk
            ctx_s[head * head_dim : (head + 1) * head_dim, :] = (
                dot(kt_s[head * head_dim : (head + 1) * head_dim, :], grad_scores) * score_scale
            ).astype(BF16)
        kcols = slice(width + cols.start, width + cols.stop)
        vcols = slice(2 * width + cols.start, 2 * width + cols.stop)
        dqkv_s[:, kcols] = key_grad.astype(BF16)
        dqkv_s[:, vcols] = value_grad.astype(BF16)
        sum_s[:, kcols] += key_grad[first:]
        sum_s[:, vcols] += value_grad[first:]
    dqkv_s[:, :width] = ctx_s[...].T
    sum_s[:, :width] += dqkv_s[first:, :width].astype(F32)
    gmid_sum_s[...] += gmid_s[first:, :]

    mid_s[...] = dot(dqkv_s[...], w_qkv[...], NT)
    for at in range(0, total, step_rows):
        part = slice(at, at + step_rows)
        unit, scale = norm_stats(rows_s[part, :])
        mid_s[part, :] = gmid_s[part, :] + norm_back(mid_s[part, :], gain1, unit, scale)
    input_grad_ref[0] = jnp.where(token_kept, mid_s[:seq, :], cot_seq_ref[0].astype(F32))

    @pl.when(image == images - 1)
    def _():
        pairs = sum_s[...]
        high = pairs.astype(BF16)
        rest = pairs - high.astype(F32)
        middle = rest.astype(BF16)
        low = (rest - middle.astype(F32)).astype(BF16)
        grad = dot(high, w_qkv[...], NT) + (
            dot(middle, w_qkv[...], NT) + dot(low, w_qkv[...], NT)
        )
        unit, scale = norm_stats(rows_s[first:, :])
        local = gmid_sum_s[...] + norm_back(grad, gain1, unit, scale)
        kept = jnp.sum(counts_ref[...].astype(F32))
        at_row = lax.broadcasted_iota(jnp.int32, local.shape, 0)
        prompt_local_ref[...] = jnp.where(at_row < prompt_count, local, kept)


def run_layer(
    tokens,
    prompts,
    keep_mask,
    counts,
    ln1_gain,
    ln1_bias,
    w_qkv,
    q_bias,
    v_bias,
    w_out,
    out_bias,
    ln2_gain,
    ln2_bias,
    w_fc1,
    fc1_bias,
    w_fc2,
    fc2_bias,
    cot_seq,
    cot_prompt,
):
    images, seq, width = tokens.shape
    prompt_count = prompts.shape[0]
    hidden = w_fc1.shape[1]
    first = round_up(seq, 8)
    total = round_up(first + prompt_count, 128)
    tail = total - first
    head_dim = width // HEADS
    row = lambda vector: vector.reshape(1, -1)
    whole = pl.BlockSpec(memory_space=pltpu.VMEM)
    anywhere = pl.BlockSpec(memory_space=pl.ANY)
    per_image = lambda shape: pl.BlockSpec((1,) + shape, lambda i: (i, 0, 0))
    return pl.pallas_call(
        layer_kernel,
        grid=(images,),
        out_shape=(
            jax.ShapeDtypeStruct((images, seq, width), BF16),
            jax.ShapeDtypeStruct((images, prompt_count, width), BF16),
            jax.ShapeDtypeStruct((images, seq, width), F32),
            jax.ShapeDtypeStruct((tail, width), F32),
        ),
        in_specs=[per_image((seq, width))]
        + [whole] * 12
        + [per_image((seq, width)), per_image((prompt_count, width))]
        + [anywhere] * 4,
        out_specs=(
            per_image((seq, width)),
            per_image((prompt_count, width)),
            per_image((seq, width)),
            whole,
        ),
        scratch_shapes=[
            pltpu.VMEM(w_qkv.shape, BF16),
            pltpu.VMEM(w_out.shape, BF16),
            pltpu.VMEM(w_fc1.shape, BF16),
            pltpu.VMEM(w_fc2.shape, BF16),
            pltpu.VMEM((total, width), F32),
            pltpu.VMEM((total, width), F32),
            pltpu.VMEM((total, width), BF16),
            pltpu.VMEM((total, width), BF16),
            pltpu.VMEM((total, width), BF16),
            pltpu.VMEM((total, width), BF16),
            pltpu.VMEM((width, total), BF16),
            pltpu.VMEM((width, total), BF16),
            pltpu.VMEM((HEADS, total, 2 * head_dim), BF16),
            pltpu.VMEM((HEADS, total, 2 * head_dim), BF16),
            pltpu.VMEM((HEADS, total, total), BF16),
            pltpu.VMEM((width, total), BF16),
            pltpu.VMEM((total, hidden), BF16),
            pltpu.VMEM((total, hidden), BF16),
            pltpu.VMEM((total, width), F32),
            pltpu.VMEM((total, width), F32),
            pltpu.VMEM((total, 3 * width), BF16),
            pltpu.VMEM((tail, 3 * width), F32),
            pltpu.VMEM((tail, width), F32),
            pltpu.SemaphoreType.DMA((4,)),
        ],
        compiler_params=pltpu.CompilerParams(vmem_limit_bytes=62 << 20),
    )(
        tokens,
        prompts,
        keep_mask,
        row(counts),
        row(ln1_gain),
        row(ln1_bias),
        row(q_bias),
        row(v_bias),
        row(out_bias),
        row(ln2_gain),
        row(ln2_bias),
        row(fc1_bias),
        row(fc2_bias),
        cot_seq,
        cot_prompt,
        w_qkv,
        w_out,
        w_fc1,
        w_fc2,
    )


def sum_kernel(
    plane, line, streams, local_ref, total_ref, sums, came, line_sums, done, send_sems, recv_sems
):
    group = plane * streams
    batch = lax.axis_index("batch")
    stream = lax.axis_index("stream")
    level = batch // plane
    spot = lax.rem(batch, plane) * streams + stream
    share = came.shape[1]
    filled = local_ref.shape[0]

    def in_plane(other):
        return (level * plane + other // streams, lax.rem(other, streams))

    def in_line(other):
        return (other * plane + lax.rem(batch, plane), stream)

    plane_peers = [lax.rem(spot + step, group) for step in range(1, group)]
    line_peers = [lax.rem(level + step, line) for step in range(1, line)]

    barrier = pltpu.get_barrier_semaphore()
    for other in plane_peers:
        pl.semaphore_signal(barrier, inc=1, device_id=in_plane(other), device_id_type=MESH)
    for other in line_peers:
        pl.semaphore_signal(barrier, inc=1, device_id=in_line(other), device_id_type=MESH)

    for at in range(group):
        low = min(at * share, filled)
        high = min((at + 1) * share, filled)
        if high > low:
            sums[at, : high - low, :] = local_ref[low:high, :]
        if high - low < share:
            sums[at, high - low :, :] = jnp.zeros((share - (high - low), sums.shape[2]), F32)
    pl.semaphore_wait(barrier, len(plane_peers) + len(line_peers))

    first_copies = []
    for step, other in enumerate(plane_peers):
        copy = pltpu.make_async_remote_copy(
            src_ref=sums.at[other],
            dst_ref=came.at[spot],
            send_sem=send_sems.at[0, step],
            recv_sem=recv_sems.at[0, spot],
            device_id=in_plane(other),
            device_id_type=MESH,
        )
        copy.start()
        first_copies.append(copy)
    came[spot] = sums[spot]
    for other in plane_peers:
        pltpu.make_async_remote_copy(
            src_ref=sums.at[other],
            dst_ref=came.at[other],
            send_sem=send_sems.at[0, 0],
            recv_sem=recv_sems.at[0, other],
            device_id=in_plane(other),
            device_id_type=MESH,
        ).wait_recv()
    part = came[0]
    for at in range(1, group):
        part = part + came[at]
    line_sums[level] = part

    second_copies = []
    for step, other in enumerate(line_peers):
        copy = pltpu.make_async_remote_copy(
            src_ref=line_sums.at[level],
            dst_ref=line_sums.at[level],
            send_sem=send_sems.at[1, step],
            recv_sem=recv_sems.at[1, level],
            device_id=in_line(other),
            device_id_type=MESH,
        )
        copy.start()
        second_copies.append(copy)
    for other in line_peers:
        pltpu.make_async_remote_copy(
            src_ref=line_sums.at[level],
            dst_ref=line_sums.at[other],
            send_sem=send_sems.at[1, 0],
            recv_sem=recv_sems.at[1, other],
            device_id=in_line(other),
            device_id_type=MESH,
        ).wait_recv()
    whole = line_sums[0]
    for at in range(1, line):
        whole = whole + line_sums[at]
    done[spot] = whole

    third_copies = []
    for step, other in enumerate(plane_peers):
        copy = pltpu.make_async_remote_copy(
            src_ref=done.at[spot],
            dst_ref=done.at[spot],
            send_sem=send_sems.at[2, step],
            recv_sem=recv_sems.at[2, spot],
            device_id=in_plane(other),
            device_id_type=MESH,
        )
        copy.start()
        third_copies.append(copy)
    for other in plane_peers:
        pltpu.make_async_remote_copy(
            src_ref=done.at[spot],
            dst_ref=done.at[other],
            send_sem=send_sems.at[2, 0],
            recv_sem=recv_sems.at[2, other],
            device_id=in_plane(other),
            device_id_type=MESH,
        ).wait_recv()
    for at in range(group):
        low = min(at * share, filled)
        high = min((at + 1) * share, filled)
        if high > low:
            total_ref[low:high, :] = done[at, : high - low, :]
    for copy in first_copies + second_copies + third_copies:
        copy.wait_send()


def sum_over_devices(local):
    devices = lax.axis_size("batch")
    streams = lax.axis_size("stream")
    plane = 2 ** math.ceil(math.log2(devices) / 2)
    line = devices // plane
    group = plane * streams
    filled, width = local.shape
    share = -(-filled // group)
    if share > 4:
        share = round_up(share, 8)
    whole = pl.BlockSpec(memory_space=pltpu.VMEM)
    return pl.pallas_call(
        functools.partial(sum_kernel, plane, line, streams),
        out_shape=jax.ShapeDtypeStruct((filled, width), F32),
        in_specs=[whole],
        out_specs=whole,
        scratch_shapes=[
            pltpu.VMEM((group, share, width), F32),
            pltpu.VMEM((group, share, width), F32),
            pltpu.VMEM((line, share, width), F32),
            pltpu.VMEM((group, share, width), F32),
            pltpu.SemaphoreType.DMA((3, max(group, line))),
            pltpu.SemaphoreType.DMA((3, max(group, line))),
        ],
        compiler_params=pltpu.CompilerParams(collective_id=0, has_side_effects=True),
    )(local)


def body(
    tokens,
    prompts,
    keep_mask,
    counts,
    ln1_gain,
    ln1_bias,
    w_qkv,
    q_bias,
    v_bias,
    w_out,
    out_bias,
    ln2_gain,
    ln2_bias,
    w_fc1,
    fc1_bias,
    w_fc2,
    fc2_bias,
    cot_seq,
    cot_prompt,
):
    images = tokens.shape[0]
    prompt_count, width = prompts.shape
    total_images = images * lax.axis_size("batch") * lax.axis_size("stream")
    layer_out, prompt_out, input_grad, prompt_local = run_layer(
        tokens,
        prompts,
        keep_mask,
        counts,
        ln1_gain,
        ln1_bias,
        w_qkv,
        q_bias,
        v_bias,
        w_out,
        out_bias,
        ln2_gain,
        ln2_bias,
        w_fc1,
        fc1_bias,
        w_fc2,
        fc2_bias,
        cot_seq,
        cot_prompt,
    )
    summed = sum_over_devices(prompt_local)
    penalty_weight = summed[prompt_count, 0] / (keep_mask.shape[1] * math.sqrt(total_images))
    prompt_grad = summed[:prompt_count] + 2.0 * penalty_weight * prompts
    penalty = penalty_weight * jnp.sum(prompts * prompts) / (prompt_count * width)
    return (layer_out, prompt_out, input_grad, prompt_grad, penalty)


def solution(mesh):
    rows = P(("batch", "stream"), None, None)
    in_specs = (
        (rows, P(), P(("batch", "stream"), None), P(("batch", "stream")))
        + (P(),) * 13
        + (rows, rows)
    )
    return jax.shard_map(
        body,
        mesh=mesh,
        in_specs=in_specs,
        out_specs=(rows, rows, rows, P(), P()),
        check_vma=False,
    )
```

time: 470 us -> 121 us (0.26); the launches traced: 463 us -> 120 us
  waiting for transfers between devices: 173 us -> 0 us
  matrix products: 112 us -> 0 us
  Pallas kernels: 0 us -> 91 us
  other arithmetic: 75.7 us -> 2.21 us
  blocking collectives: 42.2 us -> 0 us
  local copies, waits for them, and re-layouts: 41.1 us -> 23 us
  between operations: 17.9 us -> 3.78 us
    psum x2 -> x0, waiting for transfers between devices: 173 us -> none  [the longest x1 123 us: body(): prompt_total = lax.psum(prompt_local, ('batch', 'stream'))]
    dot_general x16 -> x0, matrix products: 112 us -> none  [the longest x1 19.5 us: body(): jnp.einsum('irf,df->ird', grad_hidden, w_fc1, preferred_element_type=jnp....]
    pallas_call x0 -> x2, Pallas kernels: none -> 91 us  [the longest x1 71.9 us: run_layer(): pl.pallas_call(layer_kernel, grid=(images,), out_shape=(jax.ShapeDtypeStr...]
    psum x1 -> x0, blocking collectives: 42.2 us -> none  [body(): kept_total = lax.psum(count_sum, ('batch', 'stream'))]
    another operation x2 -> x0, other arithmetic: 33.5 us -> none  [the longest x1 29 us: body(): jax.nn.gelu(rows_in, approximate=False)]
    reduce_sum x13 -> x1, other arithmetic: 16.3 us -> 2.21 us  [body(): jnp.sum(prompts * prompts)]
    convert_element_type x4 -> x0, other arithmetic: 12.6 us -> none  [the longest x1 6.93 us: body(): grad_scores = (soft_full * (grad_soft - row_dot)).astype(jnp.bfloat16)]
    slice x8 -> x1, local copies, waits for them, and re-layouts: 10.1 us -> 1.18 us  [body(): summed[prompt_count, 0] / (keep_mask.shape[1] * math.sqrt(total_images))]
  transfers between devices with their start and end apart: 2 -> 0, of which waited for: 2 -> 0; matrix products, arithmetic and copies ran while one was open for 7% -> 0% of each run, Pallas kernels for 0% -> 0%
where the time goes in v1:
time: 121 us; the launch traced here: 120 us
  Pallas kernels  91 us (75%)
  local copies, waits for them, and re-layouts  23 us (19%)
  between operations  3.78 us (3%)
  other arithmetic  2.21 us (2%)
    pallas_call x1, Pallas kernels, run_layer(): pl.pallas_call(layer_kernel, grid=(images,), out_shape=(jax.ShapeDtypeStr...  71.9 us
    pallas_call x1, Pallas kernels, sum_over_devices(): pl.pallas_call(functools.partial(sum_kernel, plane, line, streams), out_s...  19.1 us
    unnamed x14, local copies, waits for them, and re-layouts  11.6 us
    reshape x8, local copies, waits for them, and re-layouts, run_layer(): row = lambda vector: vector.reshape(1, -1)  10.2 us

profile of v1, /device:TPU:0, one launch (start us, length us, event | category | flops | bytes accessed | tf_op | source)
XLA Modules:
  0.0 120.0 jit_solution(18086549709776332012)
XLA Ops:
  0.6 1.3 %reshape.45.ln1_gain_ref = f32[1,768]{1,0:T(1,128)} reshape(f32[768]{0:T(1024)} %param.23) | data formatting | bytes 6144 | tf_op jit(solution)/shard_map/reshape | solution.py:304
  1.9 1.3 %reshape.46.ln1_bias_ref = f32[1,768]{1,0:T(1,128)} reshape(f32[768]{0:T(1024)} %param.24) | data formatting | bytes 6144 | tf_op jit(solution)/shard_map/reshape | solution.py:304
  3.2 1.3 %reshape.47.q_bias_ref = f32[1,768]{1,0:T(1,128)} reshape(f32[768]{0:T(1024)} %param.26) | data formatting | bytes 6144 | tf_op jit(solution)/shard_map/reshape | solution.py:304
  4.5 1.3 %reshape.48.v_bias_ref = f32[1,768]{1,0:T(1,128)} reshape(f32[768]{0:T(1024)} %param.27) | data formatting | bytes 6144 | tf_op jit(solution)/shard_map/reshape | solution.py:304
  5.7 1.3 %reshape.49.out_bias_ref = f32[1,768]{1,0:T(1,128)} reshape(f32[768]{0:T(1024)} %param.29) | data formatting | bytes 6144 | tf_op jit(solution)/shard_map/reshape | solution.py:304
  7.0 1.3 %reshape.50.ln2_gain_ref = f32[1,768]{1,0:T(1,128)} reshape(f32[768]{0:T(1024)} %param.30) | data formatting | bytes 6144 | tf_op jit(solution)/shard_map/reshape | solution.py:304
  8.3 1.3 %reshape.51.ln2_bias_ref = f32[1,768]{1,0:T(1,128)} reshape(f32[768]{0:T(1024)} %param.31) | data formatting | bytes 6144 | tf_op jit(solution)/shard_map/reshape | solution.py:304
  9.6 1.3 %reshape.53.fc2_bias_ref = f32[1,768]{1,0:T(1,128)} reshape(f32[768]{0:T(1024)} %param.35) | data formatting | bytes 6144 | tf_op jit(solution)/shard_map/reshape | solution.py:304
  10.9 1.7 %copy.26.cot_prompt_ref = bf16[4,50,768]{2,1,0:T(8,128)(2,1)} copy(bf16[4,50,768]{2,0,1:T(4,128)(2,1)} %param.37) | data formatting | bytes 614400 | tf_op args[18]
  12.6 2.5 %copy.24.tokens_ref = bf16[4,198,768]{2,1,0:T(8,128)(2,1)} copy(bf16[4,198,768]{2,0,1:T(4,128)(2,1)} %param.19) | data formatting | bytes 2433024 | tf_op args[0]
  15.1 0.0 copy-done.1
  15.1 1.2 copy.25.cot_seq_ref
  16.3 71.9 %shard_map.218 = (bf16[4,198,768]{2,1,0:T(8,128)(2,1)}, bf16[4,50,768]{2,1,0:T(8,128)(2,1)}, f32[4,198,768]{2,1,0:T(8,128)}, f32[56,768]{1,0:T(8,128)}) custom-call(bf16[4,198,768]{2,1,0:T(8,128)(2,1)} %copy.24.tokens_ref, f32[50,768]{1,0:T(8,128)} %prompts_ref.1, s32[4,196]{1,0:T(4,128)} %keep_ref.1, s32[1,4]{1,0:T(1,128)} %bitcast.5, ...), custom_call_target="tpu_custom_call" | custom-call | tf_op jit(solution)/shard_map/pallas_call | solution.py:308
  88.2 0.0 copy-start.2
  88.2 0.0 copy-start.3
  88.2 0.0 copy-start
  88.2 2.9 %copy.27 = bf16[4,198,768]{2,0,1:T(4,128)(2,1)} copy(bf16[4,198,768]{2,1,0:T(8,128)(2,1)} %get-tuple-element.13) | data formatting | bytes 2433024
  91.2 19.1 %shard_map.219 = f32[56,768]{1,0:T(8,128)} custom-call(f32[56,768]{1,0:T(8,128)} %get-tuple-element.12.local_ref), custom_call_target="tpu_custom_call" | custom-call | tf_op jit(solution)/shard_map/pallas_call | solution.py:506
  110.3 1.2 slice.7
  112.8 0.0 copy-done.2
  112.8 2.2 %multiply_reduce_fusion = (f32[]{:T(128)}, f32[50,768]{1,0:T(8,128)}) fusion(f32[50,768]{1,0:T(8,128)S(1)} %copy-done.2, f32[]{:T(128)} %bitcast.2, f32[56,768]{1,0:T(8,128)} %shard_map.219), kind=kLoop, calls=%fused_computation | loop fusion | flops 153599 | bytes 460808 | tf_op jit(solution)/shard_map/reduce_sum | solution.py:571
  115.7 0.0 copy-done.3
  115.7 0.8 copy.28
  116.5 2.4 %copy.29 = f32[4,198,768]{2,0,1:T(4,128)} copy(f32[4,198,768]{2,1,0:T(8,128)S(1)} %copy-done) | data formatting | bytes 4866048
  (2 shorter events, 0.0 us)
Async XLA Ops:
  12.6 2.5 %copy-start.1 = (bf16[4,198,768]{2,0,1:T(4,128)(2,1)S(1)}, bf16[4,198,768]{2,0,1:T(4,128)(2,1)}, u32[]{:S(2)}) copy-start(bf16[4,198,768]{2,0,1:T(4,128)(2,1)} %param.36) | copy-start | bytes 3649540
  88.2 24.6 %copy-start.2 = (f32[50,768]{1,0:T(8,128)S(1)}, f32[50,768]{1,0:T(8,128)}, u32[]{:S(2)}) copy-start(f32[50,768]{1,0:T(8,128)} %prompts_ref.1) | copy-start | bytes 460804
  88.2 27.4 %copy-start.3 = (bf16[4,50,768]{2,1,0:T(8,128)(2,1)S(1)}, bf16[4,50,768]{2,1,0:T(8,128)(2,1)}, u32[]{:S(2)}) copy-start(bf16[4,50,768]{2,1,0:T(8,128)(2,1)} %get-tuple-element.14) | copy-start | bytes 921604
  88.2 28.3 %copy-start = (f32[4,198,768]{2,1,0:T(8,128)S(1)}, f32[4,198,768]{2,1,0:T(8,128)}, u32[]{:S(2)}) copy-start(f32[4,198,768]{2,1,0:T(8,128)} %get-tuple-element.15) | copy-start | bytes 7299076

commit v2 on v1

--- a/solution.py
+++ b/solution.py
@@ -43,7 +43,6 @@
 
 
 def layer_kernel(
-    tokens_ref,
     prompts_ref,
     keep_ref,
     counts_ref,
@@ -56,8 +55,9 @@
     ln2_bias_ref,
     fc1_bias_ref,
     fc2_bias_ref,
-    cot_seq_ref,
-    cot_prompt_ref,
+    tokens_hbm,
+    cot_seq_hbm,
+    cot_prompt_hbm,
     w_qkv_hbm,
     w_out_hbm,
     w_fc1_hbm,
@@ -70,6 +70,14 @@
     w_out,
     w_fc1,
     w_fc2,
+    tokens_in,
+    cot_seq_in,
+    cot_prompt_in,
+    tokens_s,
+    cot_seq_s,
+    cot_prompt_s,
+    layer_s,
+    prompt_s,
     rows_s,
     cot_s,
     normed_s,
@@ -93,7 +101,7 @@
 ):
     image = pl.program_id(0)
     images = pl.num_programs(0)
-    seq, width = tokens_ref.shape[1], tokens_ref.shape[2]
+    seq, width = tokens_s.shape[0], tokens_s.shape[2]
     prompt_count = prompts_ref.shape[0]
     patches = keep_ref.shape[1]
     lead = seq - patches
@@ -107,7 +115,15 @@
     copies = [
         pltpu.make_async_copy(src, dst, sems.at[at])
         for at, (src, dst) in enumerate(
-            ((w_qkv_hbm, w_qkv), (w_out_hbm, w_out), (w_fc1_hbm, w_fc1), (w_fc2_hbm, w_fc2))
+            (
+                (tokens_hbm, tokens_in),
+                (w_qkv_hbm, w_qkv),
+                (cot_seq_hbm, cot_seq_in),
+                (cot_prompt_hbm, cot_prompt_in),
+                (w_out_hbm, w_out),
+                (w_fc1_hbm, w_fc1),
+                (w_fc2_hbm, w_fc2),
+            )
         )
     ]
 
@@ -120,6 +136,8 @@
         sum_s[...] = jnp.zeros_like(sum_s)
         gmid_sum_s[...] = jnp.zeros_like(gmid_sum_s)
         rows_s[first : first + prompt_count, :] = prompts_ref[...]
+        copies[0].wait()
+        tokens_s[...] = tokens_in[...].astype(F32)
 
     at_row = lax.broadcasted_iota(jnp.int32, (total, patches), 0)
     at_col = lax.broadcasted_iota(jnp.int32, (total, patches), 1)
@@ -133,26 +151,24 @@
     dead_add = jnp.where(live, 0.0, DEAD)
     token_kept = live[:seq]
 
-    rows_s[:seq, :] = tokens_ref[0].astype(F32)
-    cot_s[:seq, :] = jnp.where(token_kept, cot_seq_ref[0].astype(F32), 0.0)
-    cot_s[first : first + prompt_count, :] = cot_prompt_ref[0].astype(F32)
-
-    gain1 = ln1_gain_ref[...]
-    bias1 = ln1_bias_ref[...]
+    rows_s[:seq, :] = tokens_s[:, image, :]
+
+    gain1 = ln1_gain_ref[...][None, :]
+    bias1 = ln1_bias_ref[...][None, :]
     for at in range(0, total, step_rows):
         unit, _ = norm_stats(rows_s[at : at + step_rows, :])
         normed_s[at : at + step_rows, :] = (unit * gain1 + bias1).astype(BF16)
 
     @pl.when(image == 0)
     def _():
-        copies[0].wait()
+        copies[1].wait()
 
     normed = normed_s[...]
     q_s[...] = (
-        (dot(normed, w_qkv[:, :width]) + q_bias_ref[...]).astype(BF16) * jnp.asarray(score_scale, BF16)
+        (dot(normed, w_qkv[:, :width]) + q_bias_ref[...][None, :]).astype(BF16) * jnp.asarray(score_scale, BF16)
     )
     k_s[...] = dot(normed, w_qkv[:, width : 2 * width]).astype(BF16)
-    v_s[...] = (dot(normed, w_qkv[:, 2 * width :]) + v_bias_ref[...]).astype(BF16)
+    v_s[...] = (dot(normed, w_qkv[:, 2 * width :]) + v_bias_ref[...][None, :]).astype(BF16)
     kt_s[...] = k_s[...].T
     vt_s[...] = v_s[...].T
 
@@ -178,36 +194,36 @@
 
     @pl.when(image == 0)
     def _():
-        copies[1].wait()
-
+        for copy in copies[2:]:
+            copy.wait()
+        cot_seq_s[...] = cot_seq_in[...].astype(F32)
+        cot_prompt_s[...] = cot_prompt_in[...].astype(F32)
+
+    cot_s[:seq, :] = jnp.where(token_kept, cot_seq_s[:, image, :], 0.0)
+    cot_s[first : first + prompt_count, :] = cot_prompt_s[:, image, :]
     context = ctx_s[...].T
-    mid_s[...] = dot(context, w_out[...]) + out_bias_ref[...] + rows_s[...]
-    gain2 = ln2_gain_ref[...]
-    bias2 = ln2_bias_ref[...]
+    mid_s[...] = dot(context, w_out[...]) + out_bias_ref[...][None, :] + rows_s[...]
+    gain2 = ln2_gain_ref[...][None, :]
+    bias2 = ln2_bias_ref[...][None, :]
     for at in range(0, total, step_rows):
         unit, _ = norm_stats(mid_s[at : at + step_rows, :])
         normed_s[at : at + step_rows, :] = (unit * gain2 + bias2).astype(BF16)
-
-    @pl.when(image == 0)
-    def _():
-        copies[2].wait()
-        copies[3].wait()
 
     second = normed_s[...]
     grad_result = cot_s[...].astype(BF16)
     chunk = 2 * 128
     for at in range(0, hidden, chunk):
         cols = slice(at, at + chunk)
-        pre = dot(second, w_fc1[:, cols]) + fc1_bias_ref[:, cols]
+        pre = dot(second, w_fc1[:, cols]) + fc1_bias_ref[cols][None, :]
         share = 0.5 + 0.5 * lax.erf(pre * (0.5**0.5))
         density = jnp.exp(pre * pre * -0.5) * ((2.0 * math.pi) ** -0.5)
         act_s[:, cols] = (pre * share).astype(BF16)
         grad_act = dot(grad_result, w_fc2[cols, :], NT)
         gh_s[:, cols] = (grad_act * (share + pre * density)).astype(BF16)
 
-    result = dot(act_s[...], w_fc2[...]) + fc2_bias_ref[...] + mid_s[...]
-    layer_out_ref[0] = jnp.where(token_kept, result[:seq], rows_s[:seq, :]).astype(BF16)
-    prompt_out_ref[0] = result[first : first + prompt_count].astype(BF16)
+    result = dot(act_s[...], w_fc2[...]) + fc2_bias_ref[...][None, :] + mid_s[...]
+    layer_s[:, image, :] = jnp.where(token_kept, result[:seq], rows_s[:seq, :])
+    prompt_s[:, image, :] = result[first : first + prompt_count]
 
     gmid_s[...] = dot(gh_s[...], w_fc1[...], NT)
     for at in range(0, total, step_rows):
@@ -254,10 +270,12 @@
         part = slice(at, at + step_rows)
         unit, scale = norm_stats(rows_s[part, :])
         mid_s[part, :] = gmid_s[part, :] + norm_back(mid_s[part, :], gain1, unit, scale)
-    input_grad_ref[0] = jnp.where(token_kept, mid_s[:seq, :], cot_seq_ref[0].astype(F32))
+    input_grad_ref[:, image, :] = jnp.where(token_kept, mid_s[:seq, :], cot_seq_s[:, image, :])
 
     @pl.when(image == images - 1)
     def _():
+        layer_out_ref[...] = layer_s[...].astype(BF16)
+        prompt_out_ref[...] = prompt_s[...].astype(BF16)
         pairs = sum_s[...]
         high = pairs.astype(BF16)
         rest = pairs - high.astype(F32)
@@ -268,7 +286,7 @@
         )
         unit, scale = norm_stats(rows_s[first:, :])
         local = gmid_sum_s[...] + norm_back(grad, gain1, unit, scale)
-        kept = jnp.sum(counts_ref[...].astype(F32))
+        kept = jnp.sum(counts_ref[...][None, :].astype(F32))
         at_row = lax.broadcasted_iota(jnp.int32, local.shape, 0)
         prompt_local_ref[...] = jnp.where(at_row < prompt_count, local, kept)
 
@@ -301,34 +319,33 @@
     total = round_up(first + prompt_count, 128)
     tail = total - first
     head_dim = width // HEADS
-    row = lambda vector: vector.reshape(1, -1)
+    turn = lambda array: jnp.transpose(array, (1, 0, 2))
     whole = pl.BlockSpec(memory_space=pltpu.VMEM)
     anywhere = pl.BlockSpec(memory_space=pl.ANY)
-    per_image = lambda shape: pl.BlockSpec((1,) + shape, lambda i: (i, 0, 0))
-    return pl.pallas_call(
+    layer_out, prompt_out, input_grad, prompt_local = pl.pallas_call(
         layer_kernel,
         grid=(images,),
         out_shape=(
-            jax.ShapeDtypeStruct((images, seq, width), BF16),
-            jax.ShapeDtypeStruct((images, prompt_count, width), BF16),
-            jax.ShapeDtypeStruct((images, seq, width), F32),
+            jax.ShapeDtypeStruct((seq, images, width), BF16),
+            jax.ShapeDtypeStruct((prompt_count, images, width), BF16),
+            jax.ShapeDtypeStruct((seq, images, width), F32),
             jax.ShapeDtypeStruct((tail, width), F32),
         ),
-        in_specs=[per_image((seq, width))]
-        + [whole] * 12
-        + [per_image((seq, width)), per_image((prompt_count, width))]
-        + [anywhere] * 4,
-        out_specs=(
-            per_image((seq, width)),
-            per_image((prompt_count, width)),
-            per_image((seq, width)),
-            whole,
-        ),
+        in_specs=[whole] * 12 + [anywhere] * 7,
+        out_specs=(whole,) * 4,
         scratch_shapes=[
             pltpu.VMEM(w_qkv.shape, BF16),
             pltpu.VMEM(w_out.shape, BF16),
             pltpu.VMEM(w_fc1.shape, BF16),
             pltpu.VMEM(w_fc2.shape, BF16),
+            pltpu.VMEM((seq, images, width), BF16),
+            pltpu.VMEM((seq, images, width), BF16),
+            pltpu.VMEM((prompt_count, images, width), BF16),
+            pltpu.VMEM((seq, images, width), F32),
+            pltpu.VMEM((seq, images, width), F32),
+            pltpu.VMEM((prompt_count, images, width), F32),
+            pltpu.VMEM((seq, images, width), F32),
+            pltpu.VMEM((prompt_count, images, width), F32),
             pltpu.VMEM((total, width), F32),
             pltpu.VMEM((total, width), F32),
             pltpu.VMEM((total, width), BF16),
@@ -348,34 +365,49 @@
             pltpu.VMEM((total, 3 * width), BF16),
             pltpu.VMEM((tail, 3 * width), F32),
             pltpu.VMEM((tail, width), F32),
-            pltpu.SemaphoreType.DMA((4,)),
+            pltpu.SemaphoreType.DMA((7,)),
         ],
         compiler_params=pltpu.CompilerParams(vmem_limit_bytes=62 << 20),
     )(
-        tokens,
         prompts,
         keep_mask,
-        row(counts),
-        row(ln1_gain),
-        row(ln1_bias),
-        row(q_bias),
-        row(v_bias),
-        row(out_bias),
-        row(ln2_gain),
-        row(ln2_bias),
-        row(fc1_bias),
-        row(fc2_bias),
-        cot_seq,
-        cot_prompt,
+        counts,
+        ln1_gain,
+        ln1_bias,
+        q_bias,
+        v_bias,
+        out_bias,
+        ln2_gain,
+        ln2_bias,
+        fc1_bias,
+        fc2_bias,
+        turn(tokens),
+        turn(cot_seq),
+        turn(cot_prompt),
         w_qkv,
         w_out,
         w_fc1,
         w_fc2,
     )
+    return turn(layer_out), turn(prompt_out), turn(input_grad), prompt_local
 
 
 def sum_kernel(
-    plane, line, streams, local_ref, total_ref, sums, came, line_sums, done, send_sems, recv_sems
+    plane,
+    line,
+    streams,
+    patches,
+    images,
+    local_ref,
+    prompts_ref,
+    grad_ref,
+    penalty_ref,
+    sums,
+    came,
+    line_sums,
+    done,
+    send_sems,
+    recv_sems,
 ):
     group = plane * streams
     batch = lax.axis_index("batch")
@@ -407,6 +439,7 @@
             sums[at, : high - low, :] = local_ref[low:high, :]
         if high - low < share:
             sums[at, high - low :, :] = jnp.zeros((share - (high - low), sums.shape[2]), F32)
+    squares = jnp.sum(prompts_ref[...] * prompts_ref[...])
     pl.semaphore_wait(barrier, len(plane_peers) + len(line_peers))
 
     first_copies = []
@@ -483,16 +516,22 @@
             device_id=in_plane(other),
             device_id_type=MESH,
         ).wait_recv()
+    prompt_count, width = prompts_ref.shape
+    kept = done[prompt_count // share, prompt_count % share : prompt_count % share + 1, :]
+    weight = kept * (1.0 / (patches * math.sqrt(images)))
     for at in range(group):
-        low = min(at * share, filled)
-        high = min((at + 1) * share, filled)
+        low = min(at * share, prompt_count)
+        high = min((at + 1) * share, prompt_count)
         if high > low:
-            total_ref[low:high, :] = done[at, : high - low, :]
+            grad_ref[low:high, :] = (
+                done[at, : high - low, :] + 2.0 * weight * prompts_ref[low:high, :]
+            )
+    penalty_ref[...] = weight[:, :1] * (squares * (1.0 / (prompt_count * width)))
     for copy in first_copies + second_copies + third_copies:
         copy.wait_send()
 
 
-def sum_over_devices(local):
+def sum_over_devices(local, prompts, patches, images):
     devices = lax.axis_size("batch")
     streams = lax.axis_size("stream")
     plane = 2 ** math.ceil(math.log2(devices) / 2)
@@ -504,10 +543,13 @@
         share = round_up(share, 8)
     whole = pl.BlockSpec(memory_space=pltpu.VMEM)
     return pl.pallas_call(
-        functools.partial(sum_kernel, plane, line, streams),
-        out_shape=jax.ShapeDtypeStruct((filled, width), F32),
-        in_specs=[whole],
-        out_specs=whole,
+        functools.partial(sum_kernel, plane, line, streams, patches, images * devices * streams),
+        out_shape=(
+            jax.ShapeDtypeStruct(prompts.shape, F32),
+            jax.ShapeDtypeStruct((1, 1), F32),
+        ),
+        in_specs=[whole] * 2,
+        out_specs=(whole,) * 2,
         scratch_shapes=[
             pltpu.VMEM((group, share, width), F32),
             pltpu.VMEM((group, share, width), F32),
@@ -517,7 +559,7 @@
             pltpu.SemaphoreType.DMA((3, max(group, line))),
         ],
         compiler_params=pltpu.CompilerParams(collective_id=0, has_side_effects=True),
-    )(local)
+    )(local, prompts)
 
 
 def body(
@@ -541,9 +583,6 @@
     cot_seq,
     cot_prompt,
 ):
-    images = tokens.shape[0]
-    prompt_count, width = prompts.shape
-    total_images = images * lax.axis_size("batch") * lax.axis_size("stream")
     layer_out, prompt_out, input_grad, prompt_local = run_layer(
         tokens,
         prompts,
@@ -565,11 +604,10 @@
         cot_seq,
         cot_prompt,
     )
-    summed = sum_over_devices(prompt_local)
-    penalty_weight = summed[prompt_count, 0] / (keep_mask.shape[1] * math.sqrt(total_images))
-    prompt_grad = summed[:prompt_count] + 2.0 * penalty_weight * prompts
-    penalty = penalty_weight * jnp.sum(prompts * prompts) / (prompt_count * width)
-    return (layer_out, prompt_out, input_grad, prompt_grad, penalty)
+    prompt_grad, penalty = sum_over_devices(
+        prompt_local, prompts, keep_mask.shape[1], tokens.shape[0]
+    )
+    return (layer_out, prompt_out, input_grad, prompt_grad, penalty.reshape(()))
 
 
 def solution(mesh):

time: 121 us -> 99.1 us (0.82)
  local copies, waits for them, and re-layouts: 23 us -> 1.6 us
  Pallas kernels: 91 us -> 94.8 us
  other arithmetic: 2.21 us -> 0 us
  between operations: 3.78 us -> 2.42 us
    reshape x8 -> x0, local copies, waits for them, and re-layouts: 10.2 us -> none  [run_layer(): row = lambda vector: vector.reshape(1, -1)]
    unnamed x14 -> x1, local copies, waits for them, and re-layouts: 11.6 us -> 1.6 us
    pallas_call x1, Pallas kernels: 71.9 us -> 75.6 us  [run_layer(): pl.pallas_call(layer_kernel, grid=(images,), out_shape=(jax.ShapeDtypeStr...]
    reduce_sum x1 -> x0, other arithmetic: 2.21 us -> none  [body(): jnp.sum(prompts * prompts)]
where the time goes in v2:
time: 99.1 us; the launch traced here: 98.9 us
  Pallas kernels  94.8 us (96%)
  between operations  2.42 us (2%)
  local copies, waits for them, and re-layouts  1.6 us (2%)
    pallas_call x1, Pallas kernels, run_layer(): pl.pallas_call(layer_kernel, grid=(images,), out_shape=(jax.ShapeDtypeStr...  75.6 us
    pallas_call x1, Pallas kernels, sum_over_devices(): pl.pallas_call(functools.partial(sum_kernel, plane, line, streams, patche...  19.2 us

profile of v2, /device:TPU:0, one launch (start us, length us, event | category | flops | bytes accessed | tf_op | source)
XLA Modules:
  0.0 98.9 jit_solution(5064717401870954738)
XLA Ops:
  0.6 75.6 %shard_map.218 = (bf16[198,4,768]{2,1,0:T(4,128)(2,1)}, bf16[50,4,768]{2,1,0:T(4,128)(2,1)}, f32[198,4,768]{2,1,0:T(4,128)}, f32[56,768]{1,0:T(8,128)}) custom-call(f32[50,768]{1,0:T(8,128)} %prompts_ref.3, s32[4,196]{1,0:T(4,128)} %keep_ref.1, s32[4]{0:T(128)} %counts_ref.1, f32[768]{0:T(1024)} %ln1_gain_ref.1, f32[768]{0:T(1024)} %ln1_bias_ref.1, ...), custom_call_target="tpu_custom_call" | custom-call | tf_op jit(solution)/shard_map/pallas_call | solution.py:325
  76.3 19.2 %shard_map.219 = (f32[50,768]{1,0:T(8,128)}, f32[1,1]{1,0:T(1,128)}) custom-call(f32[56,768]{1,0:T(8,128)} %get-tuple-element.14.local_ref, f32[50,768]{1,0:T(8,128)} %prompts_ref.3), custom_call_target="tpu_custom_call" | custom-call | tf_op jit(solution)/shard_map/pallas_call | solution.py:545
  95.5 1.6 %copy.26 = f32[50,768]{1,0:T(8,128)} copy(f32[50,768]{1,0:T(8,128)} %get-tuple-element.25) | data formatting | bytes 307200

commit v3 on v0

v3 whole, which is shorter than its diff:
```python
import functools
import math

import jax
import jax.numpy as jnp
from jax import lax
from jax.experimental import pallas as pl
from jax.experimental.pallas import tpu as pltpu
from jax.sharding import PartitionSpec as P

HEADS = 12
EPSILON = 1e-06
F32 = jnp.float32
BF16 = jnp.bfloat16
MESH = pl.DeviceIdType.MESH
DEAD = -1e30

NN = (((1,), (0,)), ((), ()))
NT = (((1,), (1,)), ((), ()))


def dot(a, b, dims=NN):
    return lax.dot_general(a, b, dims, preferred_element_type=F32)


def round_up(value, step):
    return -(-value // step) * step


def norm_stats(rows_in):
    mean = jnp.mean(rows_in, axis=-1, keepdims=True)
    centered = rows_in - mean
    variance = jnp.mean(centered * centered, axis=-1, keepdims=True)
    scale = lax.rsqrt(variance + EPSILON)
    return centered * scale, scale


def norm_back(grad, gain, unit, scale):
    scaled = grad * gain
    mean = jnp.mean(scaled, axis=-1, keepdims=True)
    along = jnp.mean(scaled * unit, axis=-1, keepdims=True)
    return scale * (scaled - mean - unit * along)


class DeviceSum:
    def __init__(self, plane, line, streams, sums, came, line_sums, done, send_sems, recv_sems):
        self.group = plane * streams
        self.line = line
        batch = lax.axis_index("batch")
        stream = lax.axis_index("stream")
        self.level = batch // plane
        self.spot = lax.rem(batch, plane) * streams + stream
        self.sums, self.came, self.line_sums, self.done = sums, came, line_sums, done
        self.send_sems, self.recv_sems = send_sems, recv_sems
        self.in_plane = lambda other: (
            self.level * plane + other // streams,
            lax.rem(other, streams),
        )
        self.in_line = lambda other: (other * plane + lax.rem(batch, plane), stream)
        self.plane_peers = [lax.rem(self.spot + step, self.group) for step in range(1, self.group)]
        self.line_peers = [lax.rem(self.level + step, line) for step in range(1, line)]
        self.started = []

    def greet(self):
        barrier = pltpu.get_barrier_semaphore()
        for other in self.plane_peers:
            pl.semaphore_signal(
                barrier, inc=1, device_id=self.in_plane(other), device_id_type=MESH
            )
        for other in self.line_peers:
            pl.semaphore_signal(barrier, inc=1, device_id=self.in_line(other), device_id_type=MESH)

    def gather(self):
        pl.semaphore_wait(
            pltpu.get_barrier_semaphore(), len(self.plane_peers) + len(self.line_peers)
        )

    def copies(self, phase, peers, where, me, source, target):
        return [
            pltpu.make_async_remote_copy(
                src_ref=source(other),
                dst_ref=target(me),
                send_sem=self.send_sems.at[phase, step],
                recv_sem=self.recv_sems.at[phase, me],
                device_id=where(other),
                device_id_type=MESH,
            )
            for step, other in enumerate(peers)
        ]

    def send(self, phase, peers, where, me, source, target):
        started = self.copies(phase, peers, where, me, source, target)
        for copy in started:
            copy.start()
        self.started += started

    def receive(self, phase, peers, where, source, target):
        for step, other in enumerate(peers):
            pltpu.make_async_remote_copy(
                src_ref=source(other),
                dst_ref=target(other),
                send_sem=self.send_sems.at[phase, step],
                recv_sem=self.recv_sems.at[phase, other],
                device_id=where(other),
                device_id_type=MESH,
            ).wait_recv()

    def first(self):
        self.send(
            0,
            self.plane_peers,
            self.in_plane,
            self.spot,
            lambda other: self.sums.at[other],
            lambda me: self.came.at[me],
        )
        self.came[self.spot] = self.sums[self.spot]

    def second(self):
        self.receive(
            0,
            self.plane_peers,
            self.in_plane,
            lambda other: self.sums.at[other],
            lambda other: self.came.at[other],
        )
        part = self.came[0]
        for at in range(1, self.group):
            part = part + self.came[at]
        self.line_sums[self.level] = part
        self.send(
            1,
            self.line_peers,
            self.in_line,
            self.level,
            lambda other: self.line_sums.at[self.level],
            lambda me: self.line_sums.at[me],
        )

    def third(self):
        self.receive(
            1,
            self.line_peers,
            self.in_line,
            lambda other: self.line_sums.at[self.level],
            lambda other: self.line_sums.at[other],
        )
        whole = self.line_sums[0]
        for at in range(1, self.line):
            whole = whole + self.line_sums[at]
        self.done[self.spot] = whole
        self.send(
            2,
            self.plane_peers,
            self.in_plane,
            self.spot,
            lambda other: self.done.at[self.spot],
            lambda me: self.done.at[me],
        )

    def finish(self):
        self.receive(
            2,
            self.plane_peers,
            self.in_plane,
            lambda other: self.done.at[self.spot],
            lambda other: self.done.at[other],
        )
        for copy in self.started:
            copy.wait_send()


def layer_kernel(
    plane,
    line,
    streams,
    all_images,
    prompts_ref,
    keep_ref,
    counts_ref,
    ln1_gain_ref,
    ln1_bias_ref,
    q_bias_ref,
    v_bias_ref,
    out_bias_ref,
    ln2_gain_ref,
    ln2_bias_ref,
    fc1_bias_ref,
    fc2_bias_ref,
    tokens_hbm,
    cot_seq_hbm,
    cot_prompt_hbm,
    w_qkv_hbm,
    w_out_hbm,
    w_fc1_hbm,
    w_fc2_hbm,
    layer_out_hbm,
    prompt_out_hbm,
    input_grad_hbm,
    prompt_grad_ref,
    penalty_ref,
    w_qkv,
    w_out,
    w_fc1,
    w_fc2,
    seq_low,
    cot_low,
    prompt_low,
    seq_turn,
    cot_turn,
    prompt_turn,
    rows_s,
    cot_s,
    mask_s,
    live_s,
    unit1_s,
    scale1_s,
    unit2_s,
    scale2_s,
    normed_s,
    second_s,
    q_s,
    k_s,
    v_s,
    v_next,
    kt_s,
    kt_next,
    vt_s,
    qm_s,
    gm_s,
    soft_s,
    ds_s,
    ctx_s,
    gq_s,
    recip_s,
    act_s,
    gh_s,
    mid_s,
    gmid_s,
    gsec_s,
    gctx_s,
    dqkv_s,
    gnorm_s,
    igrad_s,
    igrad_rest,
    sum_s,
    gmid_sum_s,
    local_sums,
    came_sums,
    line_sums,
    done_sums,
    load_sems,
    out_sems,
    igrad_sems,
    send_sems,
    recv_sems,
):
    image = pl.program_id(0)
    images = seq_low.shape[1]
    seq, width = seq_low.shape[0], seq_low.shape[2]
    whole_rows = seq // 8 * 8
    prompt_count = prompts_ref.shape[0]
    patches = keep_ref.shape[1]
    lead = seq - patches
    head_dim = width // HEADS
    pair_dim = 2 * head_dim
    pairs = HEADS // 2
    hidden = w_fc1.shape[1]
    total = rows_s.shape[1]
    first = round_up(seq, 8)
    tail = slice(first, total)
    tail_rows = total - first
    score_scale = head_dim ** (-0.5)
    block = 32
    blocks = [slice(at, at + block) for at in range(0, total, block)]
    wide = 256
    tiles = [slice(at, at + wide) for at in range(0, width, wide)]
    past = jnp.maximum(image - 1, 0)
    coming = jnp.minimum(image + 1, images - 1)
    now2 = lax.rem(image, 2)
    other2 = 1 - now2

    gain1 = ln1_gain_ref[...][None, :]
    bias1 = ln1_bias_ref[...][None, :]
    gain2 = ln2_gain_ref[...][None, :]
    bias2 = ln2_bias_ref[...][None, :]

    lane = lax.broadcasted_iota(jnp.int32, (total, pair_dim), 1)
    low_half = lane < head_dim
    one_column = jnp.where(lane == 0, 1.0, 0.0).astype(BF16)

    loads = [
        pltpu.make_async_copy(src, dst, load_sems.at[at])
        for at, (src, dst) in enumerate(
            (
                (tokens_hbm, seq_low),
                (w_qkv_hbm, w_qkv),
                (cot_seq_hbm, cot_low),
                (cot_prompt_hbm, prompt_low),
                (w_out_hbm, w_out),
                (w_fc1_hbm, w_fc1),
                (w_fc2_hbm, w_fc2),
            )
        )
    ]
    def igrad_copies(at, slot):
        return (
            pltpu.make_async_copy(
                igrad_s.at[slot, pl.ds(0, whole_rows), :],
                input_grad_hbm.at[pl.ds(0, whole_rows), at, :],
                igrad_sems.at[0, slot],
            ),
            pltpu.make_async_copy(
                igrad_rest.at[slot],
                input_grad_hbm.at[pl.ds(whole_rows, seq - whole_rows), at, :],
                igrad_sems.at[1, slot],
            ),
        )

    def first_norm(at, slot, part):
        if part.stop <= whole_rows:
            rows = seq_turn[part, at, :]
            rows_s[slot, part, :] = rows
        else:
            if part.start < seq:
                rows_s[slot, part.start : seq, :] = seq_turn[part.start : seq, at, :]
            rows = rows_s[slot, part, :]
        unit, scale = norm_stats(rows)
        unit1_s[slot, part, :] = unit
        scale1_s[slot, part, :] = scale
        normed_s[part, :] = (unit * gain1 + bias1).astype(BF16)

    def project_query():
        q_s[...] = (dot(normed_s[...], w_qkv[:, :width]) + q_bias_ref[...][None, :]).astype(
            BF16
        ) * jnp.asarray(score_scale, BF16)

    def project_key():
        k_s[...] = dot(normed_s[...], w_qkv[:, width : 2 * width]).astype(BF16)
        kt_next[...] = k_s[...].T

    def project_value():
        value = (dot(normed_s[...], w_qkv[:, 2 * width :]) + v_bias_ref[...][None, :]).astype(BF16)
        v_next[...] = value
        for head in range(HEADS):
            vt_s[head, :head_dim, :] = value[:, head * head_dim : (head + 1) * head_dim].T

    def grad_normed(tile):
        gnorm_s[:, tile] = dot(dqkv_s[...], w_qkv[tile, :], NT)

    def first_norm_back(at, slot, part):
        grad = gmid_s[part, :] + norm_back(
            gnorm_s[part, :], gain1, unit1_s[slot, part, :], scale1_s[slot, part, :]
        )
        grad = jnp.where(live_s[at, part, :] > 0.0, grad, cot_s[slot, part, :])
        igrad_s[slot, part, :] = grad
        if part.start <= whole_rows < part.stop and seq > whole_rows:
            igrad_rest[slot] = grad[whole_rows - part.start : seq - part.start]

    over_devices = DeviceSum(
        plane, line, streams, local_sums, came_sums, line_sums, done_sums, send_sems, recv_sems
    )

    @pl.when(image == 0)
    def _():
        over_devices.greet()
        for copy in loads:
            copy.start()
        sum_s[...] = jnp.zeros_like(sum_s)
        gmid_sum_s[...] = jnp.zeros_like(gmid_sum_s)
        dqkv_s[...] = jnp.zeros_like(dqkv_s)
        gmid_s[...] = jnp.zeros_like(gmid_s)
        unit1_s[...] = jnp.zeros_like(unit1_s)
        scale1_s[...] = jnp.zeros_like(scale1_s)
        recip_s[...] = jnp.zeros_like(recip_s)
        for at in range(2):
            rows_s[at, whole_rows:, :] = jnp.zeros((total - whole_rows, width), F32)
            rows_s[at, first : first + prompt_count, :] = prompts_ref[...]
            cot_s[at, whole_rows:, :] = jnp.zeros((total - whole_rows, width), F32)
        for head in range(HEADS):
            vt_s[head, head_dim:, :] = jnp.ones((vt_s.shape[1] - head_dim, total), BF16)
        loads[0].wait()
        seq_turn[...] = seq_low[...].astype(F32)

        at_row = lax.broadcasted_iota(jnp.int32, (total, patches), 0)
        at_col = lax.broadcasted_iota(jnp.int32, (total, patches), 1)
        row_at = lax.broadcasted_iota(jnp.int32, (total, 1), 0)
        always = (row_at < lead) | ((row_at >= first) & (row_at < first + prompt_count))
        for at in range(images):
            keep_row = keep_ref[at : at + 1, :].astype(F32)
            patch_kept = jnp.sum(
                jnp.where(at_row == at_col + lead, keep_row, 0.0), axis=1, keepdims=True
            )
            live = always | (patch_kept > 0.0)
            live_s[at] = jnp.where(live, 1.0, 0.0)
            mask_s[at] = jnp.where((lane == 0) & jnp.logical_not(live), DEAD, 0.0).astype(BF16)

        for part in blocks:
            first_norm(0, 0, part)
        loads[1].wait()
        project_query()
        project_key()
        project_value()
        loads[2].wait()
        cot_turn[...] = cot_low[...].astype(F32)
        loads[3].wait()
        prompt_turn[...] = prompt_low[...].astype(F32)
        for copy in loads[4:]:
            copy.wait()

    @pl.when(image > 1)
    def _():
        for copy in igrad_copies(image - 2, now2):
            copy.start()

    v_s[...] = v_next[...]
    kt_s[...] = kt_next[...]
    mask = mask_s[image]

    def make_queries(pair):
        q_pair = q_s[:, pair * pair_dim : (pair + 1) * pair_dim]
        qm_s[pair, :total, :] = jnp.where(low_half, q_pair, jnp.zeros_like(q_pair))
        qm_s[pair, total:, :] = jnp.where(low_half, jnp.zeros_like(q_pair), q_pair)

    def head_scores(head):
        pair, half = divmod(head, 2)
        if half == 0:
            make_queries(pair)
        keys = jnp.concatenate([k_s[:, pair * pair_dim : (pair + 1) * pair_dim], mask], axis=1)
        queries = jnp.concatenate(
            [qm_s[pair, half * total : (half + 1) * total, :], one_column], axis=1
        )
        return dot(keys, queries, NT)

    scores = head_scores(0)
    for head in range(HEADS):
        pair, half = divmod(head, 2)
        current = scores
        if head + 1 < HEADS:
            scores = head_scores(head + 1)
        for at in range(0, total, 128):
            part = current[:, at : at + 128]
            top = jnp.max(part, axis=0, keepdims=True)
            soft_s[pair, :, half * total + at : half * total + at + 128] = jnp.exp(
                part - top
            ).astype(BF16)
        mixed = dot(vt_s[head], soft_s[pair, :, half * total : (half + 1) * total])
        recip = 1.0 / mixed[head_dim : head_dim + 8]
        recip_s[head : head + 1, :] = recip[:1]
        ctx_s[head * head_dim : (head + 1) * head_dim, :] = (
            mixed[:head_dim].reshape(head_dim // 8, 8, total) * recip[None]
        ).reshape(head_dim, total).astype(BF16)
        if head % 4 == 1:
            grad_normed(tiles[head // 4])

    mid_s[...] = dot(ctx_s[...].T, w_out[...]) + out_bias_ref[...][None, :] + rows_s[now2]
    for part in blocks:
        unit, scale = norm_stats(mid_s[part, :])
        unit2_s[part, :] = unit
        scale2_s[part, :] = scale
        second_s[part, :] = (unit * (0.5 * gain2) + 0.5 * bias2).astype(BF16)

    live = live_s[image]
    for part in blocks:
        if part.stop <= whole_rows:
            cot_s[now2, part, :] = cot_turn[part, image, :]
        elif part.start < seq:
            cot_s[now2, part.start : seq, :] = cot_turn[part.start : seq, image, :]
    cot_s[now2, first : first + prompt_count, :] = prompt_turn[:, image, :]
    grad_half = (jnp.where(live > 0.0, cot_s[now2], 0.0) * 0.5).astype(BF16)
    second = second_s[...]
    root2 = 2.0**0.5
    for count, at in enumerate(range(0, hidden, wide)):
        cols = slice(at, at + wide)
        half_pre = dot(second, w_fc1[:, cols]) + 0.5 * fc1_bias_ref[cols][None, :]
        grad_act = dot(grad_half, w_fc2[cols, :], NT)
        scaled = half_pre * root2
        twice = 1.0 + lax.erf(scaled)
        act_s[:, cols] = (half_pre * twice).astype(BF16)
        bell = jnp.exp2(scaled * scaled * (-math.log2(math.e)))
        gh_s[:, cols] = (grad_act * (twice + scaled * bell * (2.0 / math.pi**0.5))).astype(BF16)
        if count < len(blocks):
            first_norm_back(past, other2, blocks[count])

    per_tile = -(-len(blocks) // len(tiles))
    for count, tile in enumerate(tiles):
        gsec_s[:, tile] = dot(gh_s[...], w_fc1[tile, :], NT)
        for part in blocks[count * per_tile : (count + 1) * per_tile]:
            first_norm(coming, other2, part)
    for count, tile in enumerate(tiles):
        result = dot(act_s[...], w_fc2[:, tile]) + fc2_bias_ref[tile][None, :] + mid_s[:, tile]
        result = jnp.where(live > 0.0, result, rows_s[now2, :, tile])
        seq_turn[:, image, tile] = result[:seq]
        prompt_turn[:, image, tile] = result[first : first + prompt_count]
        for part in blocks[count * per_tile : (count + 1) * per_tile]:
            grad = jnp.where(live[part] > 0.0, cot_s[now2, part, :], 0.0)
            gmid = grad + norm_back(gsec_s[part, :], gain2, unit2_s[part, :], scale2_s[part, :])
            gmid_s[part, :] = gmid
            second_s[part, :] = gmid.astype(BF16)
    gmid_sum_s[...] += gmid_s[tail, :]

    gctx_s[...] = dot(second_s[...], w_out[...], NT)
    project_query()
    gctx_t = gctx_s[...].astype(BF16).T
    recip_t = recip_s[...].T
    for pair in range(pairs):
        cols = slice(pair * pair_dim, (pair + 1) * pair_dim)
        by_total = jnp.where(
            low_half, recip_t[:, 2 * pair : 2 * pair + 1], recip_t[:, 2 * pair + 1 : 2 * pair + 2]
        )
        scaled = (gctx_s[:, cols] * by_total).astype(BF16)
        gm_s[pair, :total, :] = jnp.where(low_half, scaled, jnp.zeros_like(scaled))
        gm_s[pair, total:, :] = jnp.where(low_half, jnp.zeros_like(scaled), scaled)
    project_key()
    project_value()

    def head_grads(head):
        pair, half = divmod(head, 2)
        return dot(
            v_s[:, pair * pair_dim : (pair + 1) * pair_dim],
            gm_s[pair, half * total : (half + 1) * total, :],
            NT,
        )

    grads = head_grads(0)
    for head in range(HEADS):
        pair, half = divmod(head, 2)
        current = grads
        if head + 1 < HEADS:
            grads = head_grads(head + 1)
        rows = slice(head * head_dim, (head + 1) * head_dim)
        row_dot = jnp.sum(
            gctx_t[rows].astype(F32) * ctx_s[rows, :].astype(F32), axis=0, keepdims=True
        ) * recip_s[head : head + 1, :]
        for at in range(0, total, 128):
            cols = slice(half * total + at, half * total + at + 128)
            ds_s[pair, :, cols] = soft_s[pair, :, cols] * (
                current[:, at : at + 128] - row_dot[:, at : at + 128]
            ).astype(BF16)
        gq_s[rows, :] = (
            dot(kt_s[rows, :], ds_s[pair, :, half * total : (half + 1) * total]) * score_scale
        ).astype(BF16)
        if half == 1:
            cols = slice(pair * pair_dim, (pair + 1) * pair_dim)
            kcols = slice(width + cols.start, width + cols.stop)
            vcols = slice(2 * width + cols.start, 2 * width + cols.stop)
            value_grad = dot(soft_s[pair], gm_s[pair])
            dqkv_s[:, vcols] = value_grad.astype(BF16)
            sum_s[:, vcols] += value_grad[first:]
            key_grad = dot(ds_s[pair], qm_s[pair])
            dqkv_s[:, kcols] = key_grad.astype(BF16)
            sum_s[:, kcols] += key_grad[first:]
    query_grad = gq_s[...].T
    dqkv_s[:, :width] = query_grad
    sum_s[:, :width] += query_grad.astype(F32)[first:]

    @pl.when(image > 1)
    def _():
        for copy in igrad_copies(image - 2, now2):
            copy.wait()

    @pl.when(image == images - 1)
    def _():
        last = images - 1
        for copy in igrad_copies(last - 1, (last - 1) % 2):
            copy.start()
        sums = sum_s[...]
        high = sums.astype(BF16)
        rest = sums - high.astype(F32)
        middle = rest.astype(BF16)
        low = (rest - middle.astype(F32)).astype(BF16)
        size = sums.shape[0]
        stacked = dot(jnp.concatenate([high, middle, low], axis=0), w_qkv[...], NT)
        grad = stacked[:size] + (stacked[size : 2 * size] + stacked[2 * size :])
        slot = last % 2
        local = gmid_sum_s[...] + norm_back(
            grad, gain1, unit1_s[slot, tail, :], scale1_s[slot, tail, :]
        )
        kept = jnp.sum(counts_ref[...][None, :].astype(F32))
        at_row = lax.broadcasted_iota(jnp.int32, local.shape, 0)
        local = jnp.where(at_row < prompt_count, local, kept)
        share = local_sums.shape[1]
        for at in range(local_sums.shape[0]):
            low_row, high_row = min(at * share, tail_rows), min((at + 1) * share, tail_rows)
            if high_row > low_row:
                local_sums[at, : high_row - low_row, :] = local[low_row:high_row]
            if high_row - low_row < share:
                local_sums[at, high_row - low_row :, :] = jnp.zeros(
                    (share - (high_row - low_row), width), F32
                )
        over_devices.gather()
        over_devices.first()
        seq_low[...] = seq_turn[...].astype(BF16)
        prompt_low[...] = prompt_turn[...].astype(BF16)
        outs = [
            pltpu.make_async_copy(seq_low, layer_out_hbm, out_sems.at[0]),
            pltpu.make_async_copy(prompt_low, prompt_out_hbm, out_sems.at[1]),
        ]
        for copy in outs:
            copy.start()
        for tile in tiles:
            grad_normed(tile)
        over_devices.second()
        for part in blocks:
            first_norm_back(last, slot, part)
        ends = igrad_copies(last, slot)
        for copy in ends:
            copy.start()
        squares = jnp.sum(prompts_ref[...] * prompts_ref[...])
        over_devices.third()
        for copy in igrad_copies(last - 1, (last - 1) % 2) + ends:
            copy.wait()
        for copy in outs:
            copy.wait()
        over_devices.finish()
        kept_row = done_sums[
            prompt_count // share, prompt_count % share : prompt_count % share + 1, :
        ]
        weight = kept_row * (1.0 / (patches * math.sqrt(all_images)))
        for at in range(done_sums.shape[0]):
            low_row, high_row = min(at * share, prompt_count), min((at + 1) * share, prompt_count)
            if high_row > low_row:
                prompt_grad_ref[low_row:high_row, :] = (
                    done_sums[at, : high_row - low_row, :]
                    + 2.0 * weight * prompts_ref[low_row:high_row, :]
                )
        penalty_ref[...] = weight[:, :1] * (squares * (1.0 / (prompt_count * width)))


def run_layer(
    tokens,
    prompts,
    keep_mask,
    counts,
    ln1_gain,
    ln1_bias,
    w_qkv,
    q_bias,
    v_bias,
    w_out,
    out_bias,
    ln2_gain,
    ln2_bias,
    w_fc1,
    fc1_bias,
    w_fc2,
    fc2_bias,
    cot_seq,
    cot_prompt,
):
    images, seq, width = tokens.shape
    prompt_count = prompts.shape[0]
    hidden = w_fc1.shape[1]
    first = round_up(seq, 8)
    total = round_up(first + prompt_count, 128)
    tail = total - first
    head_dim = width // HEADS
    pairs = HEADS // 2
    turn = lambda array: jnp.transpose(array, (1, 0, 2))
    whole = pl.BlockSpec(memory_space=pltpu.VMEM)
    anywhere = pl.BlockSpec(memory_space=pl.ANY)
    low = lambda *shape: pltpu.VMEM(shape, BF16)
    full = lambda *shape: pltpu.VMEM(shape, F32)
    devices = lax.axis_size("batch")
    streams = lax.axis_size("stream")
    plane = 2 ** math.ceil(math.log2(devices) / 2)
    line = devices // plane
    group = plane * streams
    share = -(-tail // group)
    if share > 4:
        share = round_up(share, 8)
    layer_out, prompt_out, input_grad, prompt_grad, penalty = pl.pallas_call(
        functools.partial(layer_kernel, plane, line, streams, images * devices * streams),
        grid=(images,),
        out_shape=(
            jax.ShapeDtypeStruct((seq, images, width), BF16),
            jax.ShapeDtypeStruct((prompt_count, images, width), BF16),
            jax.ShapeDtypeStruct((seq, images, width), F32),
            jax.ShapeDtypeStruct((prompt_count, width), F32),
            jax.ShapeDtypeStruct((1, 1), F32),
        ),
        in_specs=[whole] * 12 + [anywhere] * 7,
        out_specs=(anywhere,) * 3 + (whole,) * 2,
        scratch_shapes=[
            low(*w_qkv.shape),
            low(*w_out.shape),
            low(*w_fc1.shape),
            low(*w_fc2.shape),
            low(seq, images, width),
            low(seq, images, width),
            low(prompt_count, images, width),
            full(seq, images, width),
            full(seq, images, width),
            full(prompt_count, images, width),
            full(2, total, width),
            full(2, total, width),
            low(images, total, 2 * head_dim),
            full(images, total, 1),
            full(2, total, width),
            full(2, total, 1),
            full(total, width),
            full(total, 1),
            low(total, width),
            low(total, width),
            low(total, width),
            low(total, width),
            low(total, width),
            low(total, width),
            low(width, total),
            low(width, total),
            low(HEADS, head_dim + 16, total),
            low(pairs, 2 * total, 2 * head_dim),
            low(pairs, 2 * total, 2 * head_dim),
            low(pairs, total, 2 * total),
            low(pairs, total, 2 * total),
            low(width, total),
            low(width, total),
            full(16, total),
            low(total, hidden),
            low(total, hidden),
            full(total, width),
            full(total, width),
            full(total, width),
            full(total, width),
            low(total, 3 * width),
            full(total, width),
            full(2, total, width),
            full(2, max(seq % 8, 1), width),
            full(tail, 3 * width),
            full(tail, width),
            full(group, share, width),
            full(group, share, width),
            full(line, share, width),
            full(group, share, width),
            pltpu.SemaphoreType.DMA((7,)),
            pltpu.SemaphoreType.DMA((2,)),
            pltpu.SemaphoreType.DMA((2, 2)),
            pltpu.SemaphoreType.DMA((3, max(group, line))),
            pltpu.SemaphoreType.DMA((3, max(group, line))),
        ],
        compiler_params=pltpu.CompilerParams(
            vmem_limit_bytes=63 << 20, collective_id=0, has_side_effects=True
        ),
    )(
        prompts,
        keep_mask,
        counts,
        ln1_gain,
        ln1_bias,
        q_bias,
        v_bias,
        out_bias,
        ln2_gain,
        ln2_bias,
        fc1_bias,
        fc2_bias,
        turn(tokens),
        turn(cot_seq),
        turn(cot_prompt),
        w_qkv,
        w_out,
        w_fc1,
        w_fc2,
    )
    return (
        turn(layer_out),
        turn(prompt_out),
        turn(input_grad),
        prompt_grad,
        penalty.reshape(()),
    )


def solution(mesh):
    rows = P(("batch", "stream"), None, None)
    in_specs = (
        (rows, P(), P(("batch", "stream"), None), P(("batch", "stream")))
        + (P(),) * 13
        + (rows, rows)
    )
    return jax.shard_map(
        run_layer,
        mesh=mesh,
        in_specs=in_specs,
        out_specs=(rows, rows, rows, P(), P()),
        check_vma=False,
    )
```

time: 470 us -> 87.4 us (0.19); the launches traced: 463 us -> 87.2 us
  waiting for transfers between devices: 173 us -> 0 us
  matrix products: 112 us -> 0 us
  Pallas kernels: 0 us -> 78.1 us
  other arithmetic: 75.7 us -> 0 us
  blocking collectives: 42.2 us -> 0 us
  local copies, waits for them, and re-layouts: 41.1 us -> 6.77 us
  between operations: 17.9 us -> 2.4 us
    psum x2 -> x0, waiting for transfers between devices: 173 us -> none  [the longest x1 123 us: body(): prompt_total = lax.psum(prompt_local, ('batch', 'stream'))]
    dot_general x16 -> x0, matrix products: 112 us -> none  [the longest x1 19.5 us: body(): jnp.einsum('irf,df->ird', grad_hidden, w_fc1, preferred_element_type=jnp....]
    pallas_call x0 -> x1, Pallas kernels: none -> 78.1 us  [run_layer(): pl.pallas_call(functools.partial(layer_kernel, plane, line, streams, imag...]
    psum x1 -> x0, blocking collectives: 42.2 us -> none  [body(): kept_total = lax.psum(count_sum, ('batch', 'stream'))]
    another operation x2 -> x0, other arithmetic: 33.5 us -> none  [the longest x1 29 us: body(): jax.nn.gelu(rows_in, approximate=False)]
    reduce_sum x13 -> x0, other arithmetic: 16.3 us -> none  [the longest x4 4.84 us: layer_norm(): centered = values_in - row_mean]
    convert_element_type x4 -> x0, other arithmetic: 12.6 us -> none  [the longest x1 6.93 us: body(): grad_scores = (soft_full * (grad_soft - row_dot)).astype(jnp.bfloat16)]
    unnamed x89 -> x8, local copies, waits for them, and re-layouts: 18.5 us -> 6.77 us
  transfers between devices with their start and end apart: 2 -> 0, of which waited for: 2 -> 0; matrix products, arithmetic and copies ran while one was open for 7% -> 0% of each run, Pallas kernels for 0% -> 0%
where the time goes in v3:
time: 87.4 us; the launch traced here: 87.2 us
  Pallas kernels  78.1 us (89%)
  local copies, waits for them, and re-layouts  6.77 us (8%)
  between operations  2.4 us (3%)
    pallas_call x1, Pallas kernels, run_layer(): pl.pallas_call(functools.partial(layer_kernel, plane, line, streams, imag...  78.1 us
    unnamed x8, local copies, waits for them, and re-layouts  6.77 us

profile of v3, /device:TPU:0, one launch (start us, length us, event | category | flops | bytes accessed | tf_op | source)
XLA Modules:
  0.0 87.2 jit_solution(7666476589428339879)
XLA Ops:
  0.6 78.1 %shard_map.218 = (bf16[198,4,768]{2,1,0:T(4,128)(2,1)}, bf16[50,4,768]{2,1,0:T(4,128)(2,1)}, f32[198,4,768]{2,1,0:T(4,128)}, f32[50,768]{1,0:T(8,128)}, f32[1,1]{1,0:T(1,128)}) custom-call(f32[50,768]{1,0:T(8,128)} %prompts_ref.1, s32[4,196]{1,0:T(4,128)} %keep_ref.1, s32[4]{0:T(128)} %counts_ref.1, f32[768]{0:T(1024)} %ln1_gain_ref.1, f32[768]{0:T(1024)} %ln1_bias_ref.1, ...), custom_call_target="tpu_custom_call" | custom-call | tf_op jit(solution)/shard_map/pallas_call | solution.py:672
  78.7 0.0 copy-start
  78.7 2.9 %copy.29 = bf16[4,198,768]{2,0,1:T(4,128)(2,1)} copy(bf16[4,198,768]{2,0,1:T(4,128)(2,1)} %bitcast.8) | data formatting | bytes 2433024
  81.6 1.8 %copy.30 = bf16[4,50,768]{2,0,1:T(4,128)(2,1)} copy(bf16[4,50,768]{2,0,1:T(4,128)(2,1)} %bitcast.11) | data formatting | bytes 614400
  83.4 0.0 copy-done
  83.4 0.0 copy-start.1
  83.4 1.4 %copy.31 = f32[4,198,768]{2,0,1:T(4,128)} copy(f32[4,198,768]{2,0,1:T(4,128)S(1)} %bitcast.7) | data formatting | bytes 4866048
  84.8 0.0 copy-done.1
  84.8 0.7 copy.32
Async XLA Ops:
  78.7 4.7 %copy-start = (f32[198,4,768]{2,1,0:T(4,128)S(1)}, f32[198,4,768]{2,1,0:T(4,128)}, u32[]{:S(2)}) copy-start(f32[198,4,768]{2,1,0:T(4,128)} %get-tuple-element.12) | copy-start | bytes 7299076
  83.4 1.4 %copy-start.1 = (f32[50,768]{1,0:T(8,128)S(1)}, f32[50,768]{1,0:T(8,128)}, u32[]{:S(2)}) copy-start(f32[50,768]{1,0:T(8,128)} %get-tuple-element.23) | copy-start | bytes 460804

commit v4 on v3

--- a/solution.py
+++ b/solution.py
@@ -194,16 +194,15 @@
     w_out_hbm,
     w_fc1_hbm,
     w_fc2_hbm,
-    layer_out_hbm,
-    prompt_out_hbm,
-    input_grad_hbm,
+    layer_out_ref,
+    prompt_out_ref,
+    input_grad_ref,
     prompt_grad_ref,
     penalty_ref,
     w_qkv,
     w_out,
     w_fc1,
     w_fc2,
-    seq_low,
     cot_low,
     prompt_low,
     seq_turn,
@@ -213,8 +212,6 @@
     cot_s,
     mask_s,
     live_s,
-    unit1_s,
-    scale1_s,
     unit2_s,
     scale2_s,
     normed_s,
@@ -231,18 +228,17 @@
     soft_s,
     ds_s,
     ctx_s,
+    gctx_s,
     gq_s,
     recip_s,
+    half_s,
+    early_s,
     act_s,
     gh_s,
     mid_s,
     gmid_s,
-    gsec_s,
-    gctx_s,
+    grad_s,
     dqkv_s,
-    gnorm_s,
-    igrad_s,
-    igrad_rest,
     sum_s,
     gmid_sum_s,
     local_sums,
@@ -250,14 +246,11 @@
     line_sums,
     done_sums,
     load_sems,
-    out_sems,
-    igrad_sems,
     send_sems,
     recv_sems,
 ):
     image = pl.program_id(0)
-    images = seq_low.shape[1]
-    seq, width = seq_low.shape[0], seq_low.shape[2]
+    seq, images, width = layer_out_ref.shape
     whole_rows = seq // 8 * 8
     prompt_count = prompts_ref.shape[0]
     patches = keep_ref.shape[1]
@@ -275,7 +268,6 @@
     blocks = [slice(at, at + block) for at in range(0, total, block)]
     wide = 256
     tiles = [slice(at, at + wide) for at in range(0, width, wide)]
-    past = jnp.maximum(image - 1, 0)
     coming = jnp.minimum(image + 1, images - 1)
     now2 = lax.rem(image, 2)
     other2 = 1 - now2
@@ -293,7 +285,7 @@
         pltpu.make_async_copy(src, dst, load_sems.at[at])
         for at, (src, dst) in enumerate(
             (
-                (tokens_hbm, seq_low),
+                (tokens_hbm, layer_out_ref),
                 (w_qkv_hbm, w_qkv),
                 (cot_seq_hbm, cot_low),
                 (cot_prompt_hbm, prompt_low),
@@ -303,32 +295,25 @@
             )
         )
     ]
-    def igrad_copies(at, slot):
-        return (
-            pltpu.make_async_copy(
-                igrad_s.at[slot, pl.ds(0, whole_rows), :],
-                input_grad_hbm.at[pl.ds(0, whole_rows), at, :],
-                igrad_sems.at[0, slot],
-            ),
-            pltpu.make_async_copy(
-                igrad_rest.at[slot],
-                input_grad_hbm.at[pl.ds(whole_rows, seq - whole_rows), at, :],
-                igrad_sems.at[1, slot],
-            ),
-        )
+    def token_rows(source, at, target, part):
+        stop = min(part.stop, seq)
+        if stop > part.start:
+            target[part.start : stop, :] = source[part.start : stop, at, :]
+        return target[part, :]
 
     def first_norm(at, slot, part):
-        if part.stop <= whole_rows:
-            rows = seq_turn[part, at, :]
-            rows_s[slot, part, :] = rows
-        else:
-            if part.start < seq:
-                rows_s[slot, part.start : seq, :] = seq_turn[part.start : seq, at, :]
-            rows = rows_s[slot, part, :]
-        unit, scale = norm_stats(rows)
-        unit1_s[slot, part, :] = unit
-        scale1_s[slot, part, :] = scale
+        unit, _ = norm_stats(token_rows(seq_turn, at, rows_s.at[slot], part))
         normed_s[part, :] = (unit * gain1 + bias1).astype(BF16)
+
+    def result_cotangent(at, slot, part):
+        grad = token_rows(cot_turn, at, cot_s.at[slot], part)
+        low_row, high_row = max(part.start, first), min(part.stop, first + prompt_count)
+        if high_row > low_row:
+            cot_s[slot, low_row:high_row, :] = prompt_turn[low_row - first : high_row - first, at, :]
+            grad = cot_s[slot, part, :]
+        grad = jnp.where(live_s[at, part, :] > 0.0, grad, 0.0)
+        cot_s[slot, part, :] = grad
+        half_s[part, :] = (grad * 0.5).astype(BF16)
 
     def project_query():
         q_s[...] = (dot(normed_s[...], w_qkv[:, :width]) + q_bias_ref[...][None, :]).astype(
@@ -344,18 +329,6 @@
         v_next[...] = value
         for head in range(HEADS):
             vt_s[head, :head_dim, :] = value[:, head * head_dim : (head + 1) * head_dim].T
-
-    def grad_normed(tile):
-        gnorm_s[:, tile] = dot(dqkv_s[...], w_qkv[tile, :], NT)
-
-    def first_norm_back(at, slot, part):
-        grad = gmid_s[part, :] + norm_back(
-            gnorm_s[part, :], gain1, unit1_s[slot, part, :], scale1_s[slot, part, :]
-        )
-        grad = jnp.where(live_s[at, part, :] > 0.0, grad, cot_s[slot, part, :])
-        igrad_s[slot, part, :] = grad
-        if part.start <= whole_rows < part.stop and seq > whole_rows:
-            igrad_rest[slot] = grad[whole_rows - part.start : seq - part.start]
 
     over_devices = DeviceSum(
         plane, line, streams, local_sums, came_sums, line_sums, done_sums, send_sems, recv_sems
@@ -368,10 +341,6 @@
             copy.start()
         sum_s[...] = jnp.zeros_like(sum_s)
         gmid_sum_s[...] = jnp.zeros_like(gmid_sum_s)
-        dqkv_s[...] = jnp.zeros_like(dqkv_s)
-        gmid_s[...] = jnp.zeros_like(gmid_s)
-        unit1_s[...] = jnp.zeros_like(unit1_s)
-        scale1_s[...] = jnp.zeros_like(scale1_s)
         recip_s[...] = jnp.zeros_like(recip_s)
         for at in range(2):
             rows_s[at, whole_rows:, :] = jnp.zeros((total - whole_rows, width), F32)
@@ -379,9 +348,6 @@
             cot_s[at, whole_rows:, :] = jnp.zeros((total - whole_rows, width), F32)
         for head in range(HEADS):
             vt_s[head, head_dim:, :] = jnp.ones((vt_s.shape[1] - head_dim, total), BF16)
-        loads[0].wait()
-        seq_turn[...] = seq_low[...].astype(F32)
-
         at_row = lax.broadcasted_iota(jnp.int32, (total, patches), 0)
         at_col = lax.broadcasted_iota(jnp.int32, (total, patches), 1)
         row_at = lax.broadcasted_iota(jnp.int32, (total, 1), 0)
@@ -394,7 +360,8 @@
             live = always | (patch_kept > 0.0)
             live_s[at] = jnp.where(live, 1.0, 0.0)
             mask_s[at] = jnp.where((lane == 0) & jnp.logical_not(live), DEAD, 0.0).astype(BF16)
-
+        loads[0].wait()
+        seq_turn[...] = layer_out_ref[...].astype(F32)
         for part in blocks:
             first_norm(0, 0, part)
         loads[1].wait()
@@ -405,13 +372,8 @@
         cot_turn[...] = cot_low[...].astype(F32)
         loads[3].wait()
         prompt_turn[...] = prompt_low[...].astype(F32)
-        for copy in loads[4:]:
-            copy.wait()
-
-    @pl.when(image > 1)
-    def _():
-        for copy in igrad_copies(image - 2, now2):
-            copy.start()
+        for part in blocks:
+            result_cotangent(0, 0, part)
 
     v_s[...] = v_next[...]
     kt_s[...] = kt_next[...]
@@ -432,6 +394,12 @@
         )
         return dot(keys, queries, NT)
 
+    @pl.when(image == 0)
+    def _():
+        for copy in loads[4:]:
+            copy.wait()
+
+    heads_a_tile = wide // head_dim
     scores = head_scores(0)
     for head in range(HEADS):
         pair, half = divmod(head, 2)
@@ -450,69 +418,63 @@
         ctx_s[head * head_dim : (head + 1) * head_dim, :] = (
             mixed[:head_dim].reshape(head_dim // 8, 8, total) * recip[None]
         ).reshape(head_dim, total).astype(BF16)
-        if head % 4 == 1:
-            grad_normed(tiles[head // 4])
-
-    mid_s[...] = dot(ctx_s[...].T, w_out[...]) + out_bias_ref[...][None, :] + rows_s[now2]
+        if (head + 1) % heads_a_tile == 0:
+            tile = tiles[head // heads_a_tile]
+            before = mid_s[image] if tile.start else rows_s[now2] + out_bias_ref[...][None, :]
+            mid_s[image] = before + dot(ctx_s[tile, :].T, w_out[tile, :])
+
+    ahead = early_s.shape[0]
+    for count in range(ahead):
+        early_s[count] = dot(half_s[...], w_fc2[count * wide : (count + 1) * wide, :], NT)
     for part in blocks:
-        unit, scale = norm_stats(mid_s[part, :])
+        unit, scale = norm_stats(mid_s[image, part, :])
         unit2_s[part, :] = unit
         scale2_s[part, :] = scale
         second_s[part, :] = (unit * (0.5 * gain2) + 0.5 * bias2).astype(BF16)
 
-    live = live_s[image]
-    for part in blocks:
-        if part.stop <= whole_rows:
-            cot_s[now2, part, :] = cot_turn[part, image, :]
-        elif part.start < seq:
-            cot_s[now2, part.start : seq, :] = cot_turn[part.start : seq, image, :]
-    cot_s[now2, first : first + prompt_count, :] = prompt_turn[:, image, :]
-    grad_half = (jnp.where(live > 0.0, cot_s[now2], 0.0) * 0.5).astype(BF16)
     second = second_s[...]
     root2 = 2.0**0.5
     for count, at in enumerate(range(0, hidden, wide)):
         cols = slice(at, at + wide)
         half_pre = dot(second, w_fc1[:, cols]) + 0.5 * fc1_bias_ref[cols][None, :]
-        grad_act = dot(grad_half, w_fc2[cols, :], NT)
+        grad_act = early_s[count] if count < ahead else dot(half_s[...], w_fc2[cols, :], NT)
         scaled = half_pre * root2
         twice = 1.0 + lax.erf(scaled)
-        act_s[:, cols] = (half_pre * twice).astype(BF16)
+        act_s[image, :, cols] = (half_pre * twice).astype(BF16)
         bell = jnp.exp2(scaled * scaled * (-math.log2(math.e)))
         gh_s[:, cols] = (grad_act * (twice + scaled * bell * (2.0 / math.pi**0.5))).astype(BF16)
-        if count < len(blocks):
-            first_norm_back(past, other2, blocks[count])
 
     per_tile = -(-len(blocks) // len(tiles))
     for count, tile in enumerate(tiles):
-        gsec_s[:, tile] = dot(gh_s[...], w_fc1[tile, :], NT)
+        grad_s[0, :, tile] = dot(gh_s[...], w_fc1[tile, :], NT)
         for part in blocks[count * per_tile : (count + 1) * per_tile]:
             first_norm(coming, other2, part)
-    for count, tile in enumerate(tiles):
-        result = dot(act_s[...], w_fc2[:, tile]) + fc2_bias_ref[tile][None, :] + mid_s[:, tile]
-        result = jnp.where(live > 0.0, result, rows_s[now2, :, tile])
-        seq_turn[:, image, tile] = result[:seq]
-        prompt_turn[:, image, tile] = result[first : first + prompt_count]
+            result_cotangent(coming, other2, part)
+    for count, project in enumerate((project_query, project_key, project_value)):
+        project()
         for part in blocks[count * per_tile : (count + 1) * per_tile]:
-            grad = jnp.where(live[part] > 0.0, cot_s[now2, part, :], 0.0)
-            gmid = grad + norm_back(gsec_s[part, :], gain2, unit2_s[part, :], scale2_s[part, :])
-            gmid_s[part, :] = gmid
+            gmid = cot_s[now2, part, :] + norm_back(
+                grad_s[0, part, :], gain2, unit2_s[part, :], scale2_s[part, :]
+            )
+            gmid_s[image, part, :] = gmid
             second_s[part, :] = gmid.astype(BF16)
-    gmid_sum_s[...] += gmid_s[tail, :]
-
-    gctx_s[...] = dot(second_s[...], w_out[...], NT)
-    project_query()
-    gctx_t = gctx_s[...].astype(BF16).T
+    gmid_sum_s[...] += gmid_s[image, tail, :]
+
     recip_t = recip_s[...].T
-    for pair in range(pairs):
-        cols = slice(pair * pair_dim, (pair + 1) * pair_dim)
-        by_total = jnp.where(
-            low_half, recip_t[:, 2 * pair : 2 * pair + 1], recip_t[:, 2 * pair + 1 : 2 * pair + 2]
-        )
-        scaled = (gctx_s[:, cols] * by_total).astype(BF16)
-        gm_s[pair, :total, :] = jnp.where(low_half, scaled, jnp.zeros_like(scaled))
-        gm_s[pair, total:, :] = jnp.where(low_half, jnp.zeros_like(scaled), scaled)
-    project_key()
-    project_value()
+
+    def context_grads(tile):
+        grad = dot(second_s[...], w_out[tile, :], NT)
+        gctx_s[tile, :] = grad.astype(BF16).T
+        for at in range(0, wide, pair_dim):
+            pair = (tile.start + at) // pair_dim
+            by_total = jnp.where(
+                low_half,
+                recip_t[:, 2 * pair : 2 * pair + 1],
+                recip_t[:, 2 * pair + 1 : 2 * pair + 2],
+            )
+            scaled = (grad[:, at : at + pair_dim] * by_total).astype(BF16)
+            gm_s[pair, :total, :] = jnp.where(low_half, scaled, jnp.zeros_like(scaled))
+            gm_s[pair, total:, :] = jnp.where(low_half, jnp.zeros_like(scaled), scaled)
 
     def head_grads(head):
         pair, half = divmod(head, 2)
@@ -522,48 +484,44 @@
             NT,
         )
 
+    context_grads(tiles[0])
     grads = head_grads(0)
     for head in range(HEADS):
         pair, half = divmod(head, 2)
         current = grads
+        if head % heads_a_tile == 0 and head // heads_a_tile + 1 < len(tiles):
+            context_grads(tiles[head // heads_a_tile + 1])
         if head + 1 < HEADS:
             grads = head_grads(head + 1)
         rows = slice(head * head_dim, (head + 1) * head_dim)
         row_dot = jnp.sum(
-            gctx_t[rows].astype(F32) * ctx_s[rows, :].astype(F32), axis=0, keepdims=True
+            gctx_s[rows, :].astype(F32) * ctx_s[rows, :].astype(F32), axis=0, keepdims=True
         ) * recip_s[head : head + 1, :]
         for at in range(0, total, 128):
             cols = slice(half * total + at, half * total + at + 128)
-            ds_s[pair, :, cols] = soft_s[pair, :, cols] * (
+            ds_s[pair % 2, :, cols] = soft_s[pair, :, cols] * (
                 current[:, at : at + 128] - row_dot[:, at : at + 128]
             ).astype(BF16)
         gq_s[rows, :] = (
-            dot(kt_s[rows, :], ds_s[pair, :, half * total : (half + 1) * total]) * score_scale
+            dot(kt_s[rows, :], ds_s[pair % 2, :, half * total : (half + 1) * total]) * score_scale
         ).astype(BF16)
         if half == 1:
             cols = slice(pair * pair_dim, (pair + 1) * pair_dim)
             kcols = slice(width + cols.start, width + cols.stop)
             vcols = slice(2 * width + cols.start, 2 * width + cols.stop)
             value_grad = dot(soft_s[pair], gm_s[pair])
-            dqkv_s[:, vcols] = value_grad.astype(BF16)
+            dqkv_s[image, :, vcols] = value_grad.astype(BF16)
             sum_s[:, vcols] += value_grad[first:]
-            key_grad = dot(ds_s[pair], qm_s[pair])
-            dqkv_s[:, kcols] = key_grad.astype(BF16)
+            key_grad = dot(ds_s[pair % 2], qm_s[pair])
+            dqkv_s[image, :, kcols] = key_grad.astype(BF16)
             sum_s[:, kcols] += key_grad[first:]
     query_grad = gq_s[...].T
-    dqkv_s[:, :width] = query_grad
+    dqkv_s[image, :, :width] = query_grad
     sum_s[:, :width] += query_grad.astype(F32)[first:]
-
-    @pl.when(image > 1)
-    def _():
-        for copy in igrad_copies(image - 2, now2):
-            copy.wait()
 
     @pl.when(image == images - 1)
     def _():
         last = images - 1
-        for copy in igrad_copies(last - 1, (last - 1) % 2):
-            copy.start()
         sums = sum_s[...]
         high = sums.astype(BF16)
         rest = sums - high.astype(F32)
@@ -572,10 +530,8 @@
         size = sums.shape[0]
         stacked = dot(jnp.concatenate([high, middle, low], axis=0), w_qkv[...], NT)
         grad = stacked[:size] + (stacked[size : 2 * size] + stacked[2 * size :])
-        slot = last % 2
-        local = gmid_sum_s[...] + norm_back(
-            grad, gain1, unit1_s[slot, tail, :], scale1_s[slot, tail, :]
-        )
+        unit, scale = norm_stats(rows_s[0, tail, :])
+        local = gmid_sum_s[...] + norm_back(grad, gain1, unit, scale)
         kept = jnp.sum(counts_ref[...][None, :].astype(F32))
         at_row = lax.broadcasted_iota(jnp.int32, local.shape, 0)
         local = jnp.where(at_row < prompt_count, local, kept)
@@ -590,28 +546,47 @@
                 )
         over_devices.gather()
         over_devices.first()
-        seq_low[...] = seq_turn[...].astype(BF16)
-        prompt_low[...] = prompt_turn[...].astype(BF16)
-        outs = [
-            pltpu.make_async_copy(seq_low, layer_out_hbm, out_sems.at[0]),
-            pltpu.make_async_copy(prompt_low, prompt_out_hbm, out_sems.at[1]),
-        ]
-        for copy in outs:
-            copy.start()
-        for tile in tiles:
-            grad_normed(tile)
-        over_devices.second()
-        for part in blocks:
-            first_norm_back(last, slot, part)
-        ends = igrad_copies(last, slot)
-        for copy in ends:
-            copy.start()
+
+        some_rows = round_up(seq, 16)
+        token_blocks = [slice(at, min(at + block, seq)) for at in range(0, seq, block)]
+
+        def forward_out(at, tile):
+            result = dot(act_s[at], w_fc2[:, tile]) + fc2_bias_ref[tile][None, :]
+            result = result + mid_s[at, :, tile]
+            seq_turn[:, at, tile] = jnp.where(
+                live_s[at, :seq, :] > 0.0, result[:seq], seq_turn[:, at, tile]
+            )
+            prompt_turn[:, at, tile] = result[first : first + prompt_count]
+
+        def normed_grads(at):
+            for tile in tiles:
+                grad_s[at % 2, :some_rows, tile] = dot(
+                    dqkv_s[at, :some_rows, :], w_qkv[tile, :], NT
+                )
+
+        def first_norm_back(at, part):
+            unit, scale = norm_stats(seq_turn[part, at, :])
+            grad = gmid_s[at, part, :] + norm_back(grad_s[at % 2, part, :], gain1, unit, scale)
+            input_grad_ref[part, at, :] = jnp.where(
+                live_s[at, part, :] > 0.0, grad, cot_turn[part, at, :]
+            )
+
         squares = jnp.sum(prompts_ref[...] * prompts_ref[...])
-        over_devices.third()
-        for copy in igrad_copies(last - 1, (last - 1) % 2) + ends:
-            copy.wait()
-        for copy in outs:
-            copy.wait()
+        passes = {(images + 1) * 2 // 5: over_devices.second, (images + 1) * 3 // 5: over_devices.third}
+        for at in range(images + 1):
+            if at in passes:
+                passes[at]()
+            if at < images:
+                normed_grads(at)
+            for count, tile in enumerate(tiles):
+                if at > 0:
+                    forward_out(at - 1, tile)
+                if at < images:
+                    each = -(-len(token_blocks) // len(tiles))
+                    for part in token_blocks[count * each : (count + 1) * each]:
+                        first_norm_back(at, part)
+        layer_out_ref[...] = seq_turn[...].astype(BF16)
+        prompt_out_ref[...] = prompt_turn[...].astype(BF16)
         over_devices.finish()
         kept_row = done_sums[
             prompt_count // share, prompt_count % share : prompt_count % share + 1, :
@@ -673,20 +648,19 @@
         functools.partial(layer_kernel, plane, line, streams, images * devices * streams),
         grid=(images,),
         out_shape=(
-            jax.ShapeDtypeStruct((seq, images, width), BF16),
-            jax.ShapeDtypeStruct((prompt_count, images, width), BF16),
-            jax.ShapeDtypeStruct((seq, images, width), F32),
-            jax.ShapeDtypeStruct((prompt_count, width), F32),
+            low(seq, images, width),
+            low(prompt_count, images, width),
+            full(seq, images, width),
+            full(prompt_count, width),
             jax.ShapeDtypeStruct((1, 1), F32),
         ),
         in_specs=[whole] * 12 + [anywhere] * 7,
-        out_specs=(anywhere,) * 3 + (whole,) * 2,
+        out_specs=(whole,) * 5,
         scratch_shapes=[
             low(*w_qkv.shape),
             low(*w_out.shape),
             low(*w_fc1.shape),
             low(*w_fc2.shape),
-            low(seq, images, width),
             low(seq, images, width),
             low(prompt_count, images, width),
             full(seq, images, width),
@@ -696,8 +670,6 @@
             full(2, total, width),
             low(images, total, 2 * head_dim),
             full(images, total, 1),
-            full(2, total, width),
-            full(2, total, 1),
             full(total, width),
             full(total, 1),
             low(total, width),
@@ -712,20 +684,19 @@
             low(pairs, 2 * total, 2 * head_dim),
             low(pairs, 2 * total, 2 * head_dim),
             low(pairs, total, 2 * total),
-            low(pairs, total, 2 * total),
+            low(2, total, 2 * total),
+            low(width, total),
             low(width, total),
             low(width, total),
             full(16, total),
+            low(total, width),
+            full(4, total, 256),
+            low(images, total, hidden),
             low(total, hidden),
-            low(total, hidden),
-            full(total, width),
-            full(total, width),
-            full(total, width),
-            full(total, width),
-            low(total, 3 * width),
-            full(total, width),
+            full(images, total, width),
+            full(images, total, width),
             full(2, total, width),
-            full(2, max(seq % 8, 1), width),
+            low(images, total, 3 * width),
             full(tail, 3 * width),
             full(tail, width),
             full(group, share, width),
@@ -733,13 +704,11 @@
             full(line, share, width),
             full(group, share, width),
             pltpu.SemaphoreType.DMA((7,)),
-            pltpu.SemaphoreType.DMA((2,)),
-            pltpu.SemaphoreType.DMA((2, 2)),
             pltpu.SemaphoreType.DMA((3, max(group, line))),
             pltpu.SemaphoreType.DMA((3, max(group, line))),
         ],
         compiler_params=pltpu.CompilerParams(
-            vmem_limit_bytes=63 << 20, collective_id=0, has_side_effects=True
+            vmem_limit_bytes=59 << 20, collective_id=0, has_side_effects=True
         ),
     )(
         prompts,

time: 87.4 us -> 77 us (0.88)
  Pallas kernels: 78.1 us -> 70.6 us
  local copies, waits for them, and re-layouts: 6.77 us -> 3.84 us
    pallas_call x1, Pallas kernels: 78.1 us -> 70.6 us  [run_layer(): pl.pallas_call(functools.partial(layer_kernel, plane, line, streams, imag...]
    unnamed x8 -> x4, local copies, waits for them, and re-layouts: 6.77 us -> 3.84 us
where the time goes in v4:
time: 77 us; the launch traced here: 76.8 us
  Pallas kernels  70.6 us (92%)
  local copies, waits for them, and re-layouts  3.84 us (5%)
  between operations  2.34 us (3%)
    pallas_call x1, Pallas kernels, run_layer(): pl.pallas_call(functools.partial(layer_kernel, plane, line, streams, imag...  70.6 us
    unnamed x4, local copies, waits for them, and re-layouts  3.84 us

profile of v4, /device:TPU:0, one launch (start us, length us, event | category | flops | bytes accessed | tf_op | source)
XLA Modules:
  0.0 76.8 jit_solution(12502113654301709693)
XLA Ops:
  0.6 70.6 %shard_map.218 = (bf16[198,4,768]{2,1,0:T(4,128)(2,1)S(1)}, bf16[50,4,768]{2,1,0:T(4,128)(2,1)S(1)}, f32[198,4,768]{2,1,0:T(4,128)S(1)}, f32[50,768]{1,0:T(8,128)S(1)}, f32[1,1]{1,0:T(1,128)}) custom-call(f32[50,768]{1,0:T(8,128)} %prompts_ref.1, s32[4,196]{1,0:T(4,128)} %keep_ref.1, s32[4]{0:T(128)} %counts_ref.1, f32[768]{0:T(1024)} %ln1_gain_ref.1, ...), custom_call_target="tpu_custom_call" | custom-call | tf_op jit(solution)/shard_map/pallas_call | solution.py:647
  71.3 1.0 %copy.29 = bf16[4,198,768]{2,0,1:T(4,128)(2,1)} copy(bf16[4,198,768]{2,0,1:T(4,128)(2,1)S(1)} %bitcast.8) | data formatting | bytes 2433024
  72.3 0.7 copy.30
  73.0 0.7 copy.32
  73.7 1.4 %copy.31 = f32[4,198,768]{2,0,1:T(4,128)} copy(f32[4,198,768]{2,0,1:T(4,128)S(1)} %bitcast.7) | data formatting | bytes 4866048

commit v5 on v4

--- a/solution.py
+++ b/solution.py
@@ -175,6 +175,30 @@
     line,
     streams,
     all_images,
+    prompts_hbm,
+    keep_hbm,
+    counts_hbm,
+    ln1_gain_hbm,
+    ln1_bias_hbm,
+    q_bias_hbm,
+    v_bias_hbm,
+    out_bias_hbm,
+    ln2_gain_hbm,
+    ln2_bias_hbm,
+    fc1_bias_hbm,
+    fc2_bias_hbm,
+    tokens_hbm,
+    cot_seq_hbm,
+    cot_prompt_hbm,
+    w_qkv_hbm,
+    w_out_hbm,
+    w_fc1_hbm,
+    w_fc2_hbm,
+    layer_out_ref,
+    prompt_out_ref,
+    input_grad_ref,
+    prompt_grad_ref,
+    penalty_ref,
     prompts_ref,
     keep_ref,
     counts_ref,
@@ -187,18 +211,6 @@
     ln2_bias_ref,
     fc1_bias_ref,
     fc2_bias_ref,
-    tokens_hbm,
-    cot_seq_hbm,
-    cot_prompt_hbm,
-    w_qkv_hbm,
-    w_out_hbm,
-    w_fc1_hbm,
-    w_fc2_hbm,
-    layer_out_ref,
-    prompt_out_ref,
-    input_grad_ref,
-    prompt_grad_ref,
-    penalty_ref,
     w_qkv,
     w_out,
     w_fc1,
@@ -246,6 +258,7 @@
     line_sums,
     done_sums,
     load_sems,
+    small_sems,
     send_sems,
     recv_sems,
 ):
@@ -272,11 +285,6 @@
     now2 = lax.rem(image, 2)
     other2 = 1 - now2
 
-    gain1 = ln1_gain_ref[...][None, :]
-    bias1 = ln1_bias_ref[...][None, :]
-    gain2 = ln2_gain_ref[...][None, :]
-    bias2 = ln2_bias_ref[...][None, :]
-
     lane = lax.broadcasted_iota(jnp.int32, (total, pair_dim), 1)
     low_half = lane < head_dim
     one_column = jnp.where(lane == 0, 1.0, 0.0).astype(BF16)
@@ -295,6 +303,25 @@
             )
         )
     ]
+    smalls = [
+        pltpu.make_async_copy(src, dst, small_sems.at[at])
+        for at, (src, dst) in enumerate(
+            (
+                (prompts_hbm, prompts_ref),
+                (keep_hbm, keep_ref),
+                (counts_hbm, counts_ref),
+                (ln1_gain_hbm, ln1_gain_ref),
+                (ln1_bias_hbm, ln1_bias_ref),
+                (q_bias_hbm, q_bias_ref),
+                (v_bias_hbm, v_bias_ref),
+                (out_bias_hbm, out_bias_ref),
+                (ln2_gain_hbm, ln2_gain_ref),
+                (ln2_bias_hbm, ln2_bias_ref),
+                (fc1_bias_hbm, fc1_bias_ref),
+                (fc2_bias_hbm, fc2_bias_ref),
+            )
+        )
+    ]
     def token_rows(source, at, target, part):
         stop = min(part.stop, seq)
         if stop > part.start:
@@ -303,7 +330,7 @@
 
     def first_norm(at, slot, part):
         unit, _ = norm_stats(token_rows(seq_turn, at, rows_s.at[slot], part))
-        normed_s[part, :] = (unit * gain1 + bias1).astype(BF16)
+        normed_s[part, :] = (unit * ln1_gain_ref[...][None, :] + ln1_bias_ref[...][None, :]).astype(BF16)
 
     def result_cotangent(at, slot, part):
         grad = token_rows(cot_turn, at, cot_s.at[slot], part)
@@ -336,12 +363,17 @@
 
     @pl.when(image == 0)
     def _():
+        loads[0].start()
+        for copy in smalls:
+            copy.start()
+        for copy in loads[1:]:
+            copy.start()
         over_devices.greet()
-        for copy in loads:
-            copy.start()
         sum_s[...] = jnp.zeros_like(sum_s)
         gmid_sum_s[...] = jnp.zeros_like(gmid_sum_s)
         recip_s[...] = jnp.zeros_like(recip_s)
+        for copy in smalls:
+            copy.wait()
         for at in range(2):
             rows_s[at, whole_rows:, :] = jnp.zeros((total - whole_rows, width), F32)
             rows_s[at, first : first + prompt_count, :] = prompts_ref[...]
@@ -364,16 +396,15 @@
         seq_turn[...] = layer_out_ref[...].astype(F32)
         for part in blocks:
             first_norm(0, 0, part)
-        loads[1].wait()
+        for copy in loads[1:4]:
+            copy.wait()
         project_query()
+        cot_turn[...] = cot_low[...].astype(F32)
+        prompt_turn[...] = prompt_low[...].astype(F32)
         project_key()
-        project_value()
-        loads[2].wait()
-        cot_turn[...] = cot_low[...].astype(F32)
-        loads[3].wait()
-        prompt_turn[...] = prompt_low[...].astype(F32)
         for part in blocks:
             result_cotangent(0, 0, part)
+        project_value()
 
     v_s[...] = v_next[...]
     kt_s[...] = kt_next[...]
@@ -400,18 +431,18 @@
             copy.wait()
 
     heads_a_tile = wide // head_dim
-    scores = head_scores(0)
-    for head in range(HEADS):
+
+    def soften(head, scores):
         pair, half = divmod(head, 2)
-        current = scores
-        if head + 1 < HEADS:
-            scores = head_scores(head + 1)
         for at in range(0, total, 128):
-            part = current[:, at : at + 128]
+            part = scores[:, at : at + 128]
             top = jnp.max(part, axis=0, keepdims=True)
             soft_s[pair, :, half * total + at : half * total + at + 128] = jnp.exp(
                 part - top
             ).astype(BF16)
+
+    def mix(head):
+        pair, half = divmod(head, 2)
         mixed = dot(vt_s[head], soft_s[pair, :, half * total : (half + 1) * total])
         recip = 1.0 / mixed[head_dim : head_dim + 8]
         recip_s[head : head + 1, :] = recip[:1]
@@ -423,6 +454,16 @@
             before = mid_s[image] if tile.start else rows_s[now2] + out_bias_ref[...][None, :]
             mid_s[image] = before + dot(ctx_s[tile, :].T, w_out[tile, :])
 
+    before, after = 3, 3
+    waiting = [head_scores(head) for head in range(before)]
+    for head in range(HEADS + after):
+        if head + before < HEADS:
+            waiting.append(head_scores(head + before))
+        if head < HEADS:
+            soften(head, waiting.pop(0))
+        if head >= after:
+            mix(head - after)
+
     ahead = early_s.shape[0]
     for count in range(ahead):
         early_s[count] = dot(half_s[...], w_fc2[count * wide : (count + 1) * wide, :], NT)
@@ -430,7 +471,9 @@
         unit, scale = norm_stats(mid_s[image, part, :])
         unit2_s[part, :] = unit
         scale2_s[part, :] = scale
-        second_s[part, :] = (unit * (0.5 * gain2) + 0.5 * bias2).astype(BF16)
+        second_s[part, :] = (
+            unit * (0.5 * ln2_gain_ref[...][None, :]) + 0.5 * ln2_bias_ref[...][None, :]
+        ).astype(BF16)
 
     second = second_s[...]
     root2 = 2.0**0.5
@@ -450,14 +493,17 @@
         for part in blocks[count * per_tile : (count + 1) * per_tile]:
             first_norm(coming, other2, part)
             result_cotangent(coming, other2, part)
+    def second_norm_back(part):
+        gmid = cot_s[now2, part, :] + norm_back(
+            grad_s[0, part, :], ln2_gain_ref[...][None, :], unit2_s[part, :], scale2_s[part, :]
+        )
+        gmid_s[image, part, :] = gmid
+        second_s[part, :] = gmid.astype(BF16)
+
     for count, project in enumerate((project_query, project_key, project_value)):
         project()
         for part in blocks[count * per_tile : (count + 1) * per_tile]:
-            gmid = cot_s[now2, part, :] + norm_back(
-                grad_s[0, part, :], gain2, unit2_s[part, :], scale2_s[part, :]
-            )
-            gmid_s[image, part, :] = gmid
-            second_s[part, :] = gmid.astype(BF16)
+            second_norm_back(part)
     gmid_sum_s[...] += gmid_s[image, tail, :]
 
     recip_t = recip_s[...].T
@@ -484,26 +530,23 @@
             NT,
         )
 
-    context_grads(tiles[0])
-    grads = head_grads(0)
-    for head in range(HEADS):
+    def score_grads(head, grads):
         pair, half = divmod(head, 2)
-        current = grads
-        if head % heads_a_tile == 0 and head // heads_a_tile + 1 < len(tiles):
-            context_grads(tiles[head // heads_a_tile + 1])
-        if head + 1 < HEADS:
-            grads = head_grads(head + 1)
         rows = slice(head * head_dim, (head + 1) * head_dim)
         row_dot = jnp.sum(
             gctx_s[rows, :].astype(F32) * ctx_s[rows, :].astype(F32), axis=0, keepdims=True
         ) * recip_s[head : head + 1, :]
         for at in range(0, total, 128):
             cols = slice(half * total + at, half * total + at + 128)
-            ds_s[pair % 2, :, cols] = soft_s[pair, :, cols] * (
-                current[:, at : at + 128] - row_dot[:, at : at + 128]
+            ds_s[pair % 3, :, cols] = soft_s[pair, :, cols] * (
+                grads[:, at : at + 128] - row_dot[:, at : at + 128]
             ).astype(BF16)
+
+    def head_products(head):
+        pair, half = divmod(head, 2)
+        rows = slice(head * head_dim, (head + 1) * head_dim)
         gq_s[rows, :] = (
-            dot(kt_s[rows, :], ds_s[pair % 2, :, half * total : (half + 1) * total]) * score_scale
+            dot(kt_s[rows, :], ds_s[pair % 3, :, half * total : (half + 1) * total]) * score_scale
         ).astype(BF16)
         if half == 1:
             cols = slice(pair * pair_dim, (pair + 1) * pair_dim)
@@ -512,9 +555,22 @@
             value_grad = dot(soft_s[pair], gm_s[pair])
             dqkv_s[image, :, vcols] = value_grad.astype(BF16)
             sum_s[:, vcols] += value_grad[first:]
-            key_grad = dot(ds_s[pair % 2], qm_s[pair])
+            key_grad = dot(ds_s[pair % 3], qm_s[pair])
             dqkv_s[image, :, kcols] = key_grad.astype(BF16)
             sum_s[:, kcols] += key_grad[first:]
+
+    context_grads(tiles[0])
+    before, after = 2, 3
+    waiting = [head_grads(head) for head in range(before)]
+    for head in range(HEADS + after):
+        if head % heads_a_tile == 0 and head // heads_a_tile + 1 < len(tiles):
+            context_grads(tiles[head // heads_a_tile + 1])
+        if head + before < HEADS:
+            waiting.append(head_grads(head + before))
+        if head < HEADS:
+            score_grads(head, waiting.pop(0))
+        if head >= after:
+            head_products(head - after)
     query_grad = gq_s[...].T
     dqkv_s[image, :, :width] = query_grad
     sum_s[:, :width] += query_grad.astype(F32)[first:]
@@ -531,7 +587,7 @@
         stacked = dot(jnp.concatenate([high, middle, low], axis=0), w_qkv[...], NT)
         grad = stacked[:size] + (stacked[size : 2 * size] + stacked[2 * size :])
         unit, scale = norm_stats(rows_s[0, tail, :])
-        local = gmid_sum_s[...] + norm_back(grad, gain1, unit, scale)
+        local = gmid_sum_s[...] + norm_back(grad, ln1_gain_ref[...][None, :], unit, scale)
         kept = jnp.sum(counts_ref[...][None, :].astype(F32))
         at_row = lax.broadcasted_iota(jnp.int32, local.shape, 0)
         local = jnp.where(at_row < prompt_count, local, kept)
@@ -566,7 +622,7 @@
 
         def first_norm_back(at, part):
             unit, scale = norm_stats(seq_turn[part, at, :])
-            grad = gmid_s[at, part, :] + norm_back(grad_s[at % 2, part, :], gain1, unit, scale)
+            grad = gmid_s[at, part, :] + norm_back(grad_s[at % 2, part, :], ln1_gain_ref[...][None, :], unit, scale)
             input_grad_ref[part, at, :] = jnp.where(
                 live_s[at, part, :] > 0.0, grad, cot_turn[part, at, :]
             )
@@ -600,6 +656,18 @@
                     + 2.0 * weight * prompts_ref[low_row:high_row, :]
                 )
         penalty_ref[...] = weight[:, :1] * (squares * (1.0 / (prompt_count * width)))
+
+
+def write_kernel(*refs):
+    sems = refs[-1]
+    count = len(refs) // 2
+    copies = [
+        pltpu.make_async_copy(refs[at], refs[count + at], sems.at[at]) for at in range(count)
+    ]
+    for copy in copies:
+        copy.start()
+    for copy in copies:
+        copy.wait()
 
 
 def run_layer(
@@ -652,11 +720,30 @@
             low(prompt_count, images, width),
             full(seq, images, width),
             full(prompt_count, width),
-            jax.ShapeDtypeStruct((1, 1), F32),
+            full(1, 1),
         ),
-        in_specs=[whole] * 12 + [anywhere] * 7,
+        in_specs=[anywhere] * 19,
         out_specs=(whole,) * 5,
         scratch_shapes=[
+            full(*prompts.shape),
+            pltpu.VMEM(keep_mask.shape, jnp.int32),
+            pltpu.VMEM(counts.shape, jnp.int32),
+        ]
+        + [
+            full(*vector.shape)
+            for vector in (
+                ln1_gain,
+                ln1_bias,
+                q_bias,
+                v_bias,
+                out_bias,
+                ln2_gain,
+                ln2_bias,
+                fc1_bias,
+                fc2_bias,
+            )
+        ]
+        + [
             low(*w_qkv.shape),
             low(*w_out.shape),
             low(*w_fc1.shape),
@@ -684,7 +771,7 @@
             low(pairs, 2 * total, 2 * head_dim),
             low(pairs, 2 * total, 2 * head_dim),
             low(pairs, total, 2 * total),
-            low(2, total, 2 * total),
+            low(3, total, 2 * total),
             low(width, total),
             low(width, total),
             low(width, total),
@@ -704,6 +791,7 @@
             full(line, share, width),
             full(group, share, width),
             pltpu.SemaphoreType.DMA((7,)),
+            pltpu.SemaphoreType.DMA((12,)),
             pltpu.SemaphoreType.DMA((3, max(group, line))),
             pltpu.SemaphoreType.DMA((3, max(group, line))),
         ],
@@ -731,6 +819,18 @@
         w_fc1,
         w_fc2,
     )
+    results = tuple(
+        pltpu.with_memory_space_constraint(item, pltpu.VMEM)
+        for item in (layer_out, prompt_out, input_grad, prompt_grad, penalty)
+    )
+    layer_out, prompt_out, input_grad, prompt_grad, penalty = pl.pallas_call(
+        write_kernel,
+        out_shape=tuple(jax.ShapeDtypeStruct(item.shape, item.dtype) for item in results),
+        in_specs=[whole] * len(results),
+        out_specs=(anywhere,) * len(results),
+        scratch_shapes=[pltpu.SemaphoreType.DMA((len(results),))],
+        compiler_params=pltpu.CompilerParams(vmem_limit_bytes=1 << 20),
+    )(*results)
     return (
         turn(layer_out),
         turn(prompt_out),

time: 77 us -> 69.3 us (0.90)
  local copies, waits for them, and re-layouts: 3.84 us -> 0 us
  Pallas kernels: 70.6 us -> 68.5 us
  between operations: 2.34 us -> 0.65 us
    pallas_call x1, Pallas kernels: 70.6 us -> 65.9 us  [run_layer(): pl.pallas_call(functools.partial(layer_kernel, plane, line, streams, imag...]
    unnamed x4 -> x0, local copies, waits for them, and re-layouts: 3.84 us -> none
    pallas_call x0 -> x1, Pallas kernels: none -> 2.65 us  [run_layer(): pl.pallas_call(write_kernel, out_shape=tuple((jax.ShapeDtypeStruct(item.s...]
where the time goes in v5:
time: 69.3 us; the launch traced here: 69.2 us
  Pallas kernels  68.5 us (99%)
    pallas_call x1, Pallas kernels, run_layer(): pl.pallas_call(functools.partial(layer_kernel, plane, line, streams, imag...  65.9 us
    pallas_call x1, Pallas kernels, run_layer(): pl.pallas_call(write_kernel, out_shape=tuple((jax.ShapeDtypeStruct(item.s...  2.65 us

profile of v5, /device:TPU:0, one launch (start us, length us, event | category | flops | bytes accessed | tf_op | source)
XLA Modules:
  0.0 69.2 jit_solution(14873531681352746952)
XLA Ops:
  0.6 65.9 %shard_map.218 = (bf16[198,4,768]{2,1,0:T(4,128)(2,1)S(1)}, bf16[50,4,768]{2,1,0:T(4,128)(2,1)S(1)}, f32[198,4,768]{2,1,0:T(4,128)S(1)}, f32[50,768]{1,0:T(8,128)S(1)}, f32[1,1]{1,0:T(1,128)}) custom-call(f32[50,768]{1,0:T(8,128)} %prompts_hbm.1, s32[4,196]{1,0:T(4,128)} %keep_hbm.1, s32[4]{0:T(128)} %counts_hbm.1, f32[768]{0:T(1024)} %ln1_gain_hbm.1, ...), custom_call_target="tpu_custom_call" | custom-call | tf_op jit(solution)/shard_map/pallas_call | solution.py:715
  66.5 2.6 %shard_map.219 = (bf16[198,4,768]{2,1,0:T(4,128)(2,1)}, bf16[50,4,768]{2,1,0:T(4,128)(2,1)}, f32[198,4,768]{2,1,0:T(4,128)}, f32[50,768]{1,0:T(8,128)}, f32[1,1]{1,0:T(1,128)}) custom-call(bf16[198,4,768]{2,1,0:T(4,128)(2,1)S(1)} %get-tuple-element.15.refs_0_, bf16[50,4,768]{2,1,0:T(4,128)(2,1)S(1)} %get-tuple-element.16.refs_1_, ...), custom_call_target="tpu_custom_call" | custom-call | tf_op jit(solution)/shard_map/pallas_call | solution.py:826

commit v6 on v5

--- a/solution.py
+++ b/solution.py
@@ -294,12 +294,14 @@
         for at, (src, dst) in enumerate(
             (
                 (tokens_hbm, layer_out_ref),
-                (w_qkv_hbm, w_qkv),
+                (w_qkv_hbm.at[:, pl.ds(0, width)], w_qkv.at[:, pl.ds(0, width)]),
+                (w_qkv_hbm.at[:, pl.ds(width, width)], w_qkv.at[:, pl.ds(width, width)]),
+                (w_qkv_hbm.at[:, pl.ds(2 * width, width)], w_qkv.at[:, pl.ds(2 * width, width)]),
                 (cot_seq_hbm, cot_low),
                 (cot_prompt_hbm, prompt_low),
                 (w_out_hbm, w_out),
+                (w_fc2_hbm, w_fc2),
                 (w_fc1_hbm, w_fc1),
-                (w_fc2_hbm, w_fc2),
             )
         )
     ]
@@ -342,18 +344,22 @@
         cot_s[slot, part, :] = grad
         half_s[part, :] = (grad * 0.5).astype(BF16)
 
-    def project_query():
-        q_s[...] = (dot(normed_s[...], w_qkv[:, :width]) + q_bias_ref[...][None, :]).astype(
-            BF16
-        ) * jnp.asarray(score_scale, BF16)
-
-    def project_key():
-        k_s[...] = dot(normed_s[...], w_qkv[:, width : 2 * width]).astype(BF16)
+    some_rows = round_up(seq, 16)
+
+    def project_query(stop):
+        q_s[:stop, :] = (
+            dot(normed_s[:stop, :], w_qkv[:, :width]) + q_bias_ref[...][None, :]
+        ).astype(BF16) * jnp.asarray(score_scale, BF16)
+
+    def project_key(stop):
+        k_s[:stop, :] = dot(normed_s[:stop, :], w_qkv[:, width : 2 * width]).astype(BF16)
         kt_next[...] = k_s[...].T
 
-    def project_value():
-        value = (dot(normed_s[...], w_qkv[:, 2 * width :]) + v_bias_ref[...][None, :]).astype(BF16)
-        v_next[...] = value
+    def project_value(stop):
+        v_next[:stop, :] = (
+            dot(normed_s[:stop, :], w_qkv[:, 2 * width :]) + v_bias_ref[...][None, :]
+        ).astype(BF16)
+        value = v_next[...]
         for head in range(HEADS):
             vt_s[head, :head_dim, :] = value[:, head * head_dim : (head + 1) * head_dim].T
 
@@ -366,7 +372,7 @@
         loads[0].start()
         for copy in smalls:
             copy.start()
-        for copy in loads[1:]:
+        for copy in loads[1:6]:
             copy.start()
         over_devices.greet()
         sum_s[...] = jnp.zeros_like(sum_s)
@@ -393,18 +399,23 @@
             live_s[at] = jnp.where(live, 1.0, 0.0)
             mask_s[at] = jnp.where((lane == 0) & jnp.logical_not(live), DEAD, 0.0).astype(BF16)
         loads[0].wait()
+        for copy in loads[6:]:
+            copy.start()
         seq_turn[...] = layer_out_ref[...].astype(F32)
         for part in blocks:
             first_norm(0, 0, part)
-        for copy in loads[1:4]:
+        loads[1].wait()
+        project_query(total)
+        loads[2].wait()
+        project_key(total)
+        loads[3].wait()
+        for copy in loads[4:6]:
             copy.wait()
-        project_query()
         cot_turn[...] = cot_low[...].astype(F32)
         prompt_turn[...] = prompt_low[...].astype(F32)
-        project_key()
+        project_value(total)
         for part in blocks:
             result_cotangent(0, 0, part)
-        project_value()
 
     v_s[...] = v_next[...]
     kt_s[...] = kt_next[...]
@@ -427,8 +438,7 @@
 
     @pl.when(image == 0)
     def _():
-        for copy in loads[4:]:
-            copy.wait()
+        loads[6].wait()
 
     heads_a_tile = wide // head_dim
 
@@ -464,16 +474,22 @@
         if head >= after:
             mix(head - after)
 
+    @pl.when(image == 0)
+    def _():
+        for copy in loads[7:]:
+            copy.wait()
+
     ahead = early_s.shape[0]
     for count in range(ahead):
         early_s[count] = dot(half_s[...], w_fc2[count * wide : (count + 1) * wide, :], NT)
-    for part in blocks:
-        unit, scale = norm_stats(mid_s[image, part, :])
-        unit2_s[part, :] = unit
-        scale2_s[part, :] = scale
-        second_s[part, :] = (
-            unit * (0.5 * ln2_gain_ref[...][None, :]) + 0.5 * ln2_bias_ref[...][None, :]
-        ).astype(BF16)
+        share_of = -(-len(blocks) // ahead)
+        for part in blocks[count * share_of : (count + 1) * share_of]:
+            unit, scale = norm_stats(mid_s[image, part, :])
+            unit2_s[part, :] = unit
+            scale2_s[part, :] = scale
+            second_s[part, :] = (
+                unit * (0.5 * ln2_gain_ref[...][None, :]) + 0.5 * ln2_bias_ref[...][None, :]
+            ).astype(BF16)
 
     second = second_s[...]
     root2 = 2.0**0.5
@@ -491,7 +507,8 @@
     for count, tile in enumerate(tiles):
         grad_s[0, :, tile] = dot(gh_s[...], w_fc1[tile, :], NT)
         for part in blocks[count * per_tile : (count + 1) * per_tile]:
-            first_norm(coming, other2, part)
+            if part.start < some_rows:
+                first_norm(coming, other2, part)
             result_cotangent(coming, other2, part)
     def second_norm_back(part):
         gmid = cot_s[now2, part, :] + norm_back(
@@ -501,7 +518,7 @@
         second_s[part, :] = gmid.astype(BF16)
 
     for count, project in enumerate((project_query, project_key, project_value)):
-        project()
+        project(some_rows)
         for part in blocks[count * per_tile : (count + 1) * per_tile]:
             second_norm_back(part)
     gmid_sum_s[...] += gmid_s[image, tail, :]
@@ -603,44 +620,55 @@
         over_devices.gather()
         over_devices.first()
 
-        some_rows = round_up(seq, 16)
         token_blocks = [slice(at, min(at + block, seq)) for at in range(0, seq, block)]
 
-        def forward_out(at, tile):
-            result = dot(act_s[at], w_fc2[:, tile]) + fc2_bias_ref[tile][None, :]
-            result = result + mid_s[at, :, tile]
-            seq_turn[:, at, tile] = jnp.where(
-                live_s[at, :seq, :] > 0.0, result[:seq], seq_turn[:, at, tile]
-            )
-            prompt_turn[:, at, tile] = result[first : first + prompt_count]
-
-        def normed_grads(at):
+        def forward_out(group, tile):
+            count = len(group)
+            products = dot(
+                act_s[group[0] : group[0] + count].reshape(count * total, hidden), w_fc2[:, tile]
+            )
+            for order, at in enumerate(group):
+                result = products[order * total : (order + 1) * total]
+                result = result + fc2_bias_ref[tile][None, :] + mid_s[at, :, tile]
+                seq_turn[:, at, tile] = jnp.where(
+                    live_s[at, :seq, :] > 0.0, result[:seq], seq_turn[:, at, tile]
+                )
+                prompt_turn[:, at, tile] = result[first : first + prompt_count]
+
+        def normed_grads(group):
+            count = len(group)
+            grads = dqkv_s[group[0] : group[0] + count, :some_rows, :]
             for tile in tiles:
-                grad_s[at % 2, :some_rows, tile] = dot(
-                    dqkv_s[at, :some_rows, :], w_qkv[tile, :], NT
-                )
-
-        def first_norm_back(at, part):
-            unit, scale = norm_stats(seq_turn[part, at, :])
-            grad = gmid_s[at, part, :] + norm_back(grad_s[at % 2, part, :], ln1_gain_ref[...][None, :], unit, scale)
+                grad_s[:count, :some_rows, tile] = dot(
+                    grads.reshape(count * some_rows, 3 * width), w_qkv[tile, :], NT
+                ).reshape(count, some_rows, wide)
+
+        def first_norm_back(at, order, part):
+            unit, scale = norm_stats(layer_out_ref[part, at, :].astype(F32))
+            grad = gmid_s[at, part, :] + norm_back(
+                grad_s[order, part, :], ln1_gain_ref[...][None, :], unit, scale
+            )
             input_grad_ref[part, at, :] = jnp.where(
                 live_s[at, part, :] > 0.0, grad, cot_turn[part, at, :]
             )
 
         squares = jnp.sum(prompts_ref[...] * prompts_ref[...])
-        passes = {(images + 1) * 2 // 5: over_devices.second, (images + 1) * 3 // 5: over_devices.third}
-        for at in range(images + 1):
-            if at in passes:
-                passes[at]()
-            if at < images:
-                normed_grads(at)
+        groups = [list(range(at, min(at + 2, images))) for at in range(0, images, 2)]
+        spots = len(groups) * len(tiles)
+        passes = {spots * 2 // 6: over_devices.second, spots * 4 // 6: over_devices.third}
+        for turn_at, group in enumerate(groups):
+            todo = [
+                (at, order, part) for order, at in enumerate(group) for part in token_blocks
+            ]
+            each = -(-len(todo) // len(tiles))
             for count, tile in enumerate(tiles):
-                if at > 0:
-                    forward_out(at - 1, tile)
-                if at < images:
-                    each = -(-len(token_blocks) // len(tiles))
-                    for part in token_blocks[count * each : (count + 1) * each]:
-                        first_norm_back(at, part)
+                if turn_at * len(tiles) + count in passes:
+                    passes[turn_at * len(tiles) + count]()
+                if count == 0:
+                    normed_grads(group)
+                forward_out(group, tile)
+                for item in todo[count * each : (count + 1) * each]:
+                    first_norm_back(*item)
         layer_out_ref[...] = seq_turn[...].astype(BF16)
         prompt_out_ref[...] = prompt_turn[...].astype(BF16)
         over_devices.finish()
@@ -661,9 +689,17 @@
 def write_kernel(*refs):
     sems = refs[-1]
     count = len(refs) // 2
-    copies = [
-        pltpu.make_async_copy(refs[at], refs[count + at], sems.at[at]) for at in range(count)
-    ]
+    copies = []
+    for at in range(count):
+        size = refs[at].shape[0]
+        cuts = 4 if size > 100 else 1
+        for cut in range(cuts):
+            part = pl.ds(cut * size // cuts, (cut + 1) * size // cuts - cut * size // cuts)
+            copies.append(
+                pltpu.make_async_copy(
+                    refs[at].at[part], refs[count + at].at[part], sems.at[at, cut]
+                )
+            )
     for copy in copies:
         copy.start()
     for copy in copies:
@@ -790,7 +826,7 @@
             full(group, share, width),
             full(line, share, width),
             full(group, share, width),
-            pltpu.SemaphoreType.DMA((7,)),
+            pltpu.SemaphoreType.DMA((9,)),
             pltpu.SemaphoreType.DMA((12,)),
             pltpu.SemaphoreType.DMA((3, max(group, line))),
             pltpu.SemaphoreType.DMA((3, max(group, line))),
@@ -828,7 +864,7 @@
         out_shape=tuple(jax.ShapeDtypeStruct(item.shape, item.dtype) for item in results),
         in_specs=[whole] * len(results),
         out_specs=(anywhere,) * len(results),
-        scratch_shapes=[pltpu.SemaphoreType.DMA((len(results),))],
+        scratch_shapes=[pltpu.SemaphoreType.DMA((len(results), 4))],
         compiler_params=pltpu.CompilerParams(vmem_limit_bytes=1 << 20),
     )(*results)
     return (

time: 69.3 us -> 67.5 us (0.974)
  Pallas kernels: 68.5 us -> 66.6 us
    pallas_call x1, Pallas kernels: 65.9 us -> 63.9 us  [run_layer(): pl.pallas_call(functools.partial(layer_kernel, plane, line, streams, imag...]
where the time goes in v6:
time: 67.5 us; the launch traced here: 67.3 us
  Pallas kernels  66.6 us (99%)
    pallas_call x1, Pallas kernels, run_layer(): pl.pallas_call(functools.partial(layer_kernel, plane, line, streams, imag...  63.9 us
    pallas_call x1, Pallas kernels, run_layer(): pl.pallas_call(write_kernel, out_shape=tuple((jax.ShapeDtypeStruct(item.s...  2.78 us

profile of v6, /device:TPU:0, one launch (start us, length us, event | category | flops | bytes accessed | tf_op | source)
XLA Modules:
  0.0 67.3 jit_solution(10316666579789268947)
XLA Ops:
  0.6 63.9 %shard_map.218 = (bf16[198,4,768]{2,1,0:T(4,128)(2,1)S(1)}, bf16[50,4,768]{2,1,0:T(4,128)(2,1)S(1)}, f32[198,4,768]{2,1,0:T(4,128)S(1)}, f32[50,768]{1,0:T(8,128)S(1)}, f32[1,1]{1,0:T(1,128)}) custom-call(f32[50,768]{1,0:T(8,128)} %prompts_hbm.1, s32[4,196]{1,0:T(4,128)} %keep_hbm.1, s32[4]{0:T(128)} %counts_hbm.1, f32[768]{0:T(1024)} %ln1_gain_hbm.1, ...), custom_call_target="tpu_custom_call" | custom-call | tf_op jit(solution)/shard_map/pallas_call | solution.py:751
  64.5 2.8 %shard_map.219 = (bf16[198,4,768]{2,1,0:T(4,128)(2,1)}, bf16[50,4,768]{2,1,0:T(4,128)(2,1)}, f32[198,4,768]{2,1,0:T(4,128)}, f32[50,768]{1,0:T(8,128)}, f32[1,1]{1,0:T(1,128)}) custom-call(bf16[198,4,768]{2,1,0:T(4,128)(2,1)S(1)} %get-tuple-element.15.refs_0_, bf16[50,4,768]{2,1,0:T(4,128)(2,1)S(1)} %get-tuple-element.16.refs_1_, ...), custom_call_target="tpu_custom_call" | custom-call | tf_op jit(solution)/shard_map/pallas_call | solution.py:862

commit v7 on v6

--- a/solution.py
+++ b/solution.py
@@ -240,7 +240,8 @@
     soft_s,
     ds_s,
     ctx_s,
-    gctx_s,
+    gmt_s,
+    mixed_s,
     gq_s,
     recip_s,
     half_s,
@@ -456,6 +457,7 @@
         mixed = dot(vt_s[head], soft_s[pair, :, half * total : (half + 1) * total])
         recip = 1.0 / mixed[head_dim : head_dim + 8]
         recip_s[head : head + 1, :] = recip[:1]
+        mixed_s[head * head_dim : (head + 1) * head_dim, :] = mixed[:head_dim]
         ctx_s[head * head_dim : (head + 1) * head_dim, :] = (
             mixed[:head_dim].reshape(head_dim // 8, 8, total) * recip[None]
         ).reshape(head_dim, total).astype(BF16)
@@ -527,7 +529,6 @@
 
     def context_grads(tile):
         grad = dot(second_s[...], w_out[tile, :], NT)
-        gctx_s[tile, :] = grad.astype(BF16).T
         for at in range(0, wide, pair_dim):
             pair = (tile.start + at) // pair_dim
             by_total = jnp.where(
@@ -536,6 +537,7 @@
                 recip_t[:, 2 * pair + 1 : 2 * pair + 2],
             )
             scaled = (grad[:, at : at + pair_dim] * by_total).astype(BF16)
+            gmt_s[tile.start + at : tile.start + at + pair_dim, :] = scaled.T
             gm_s[pair, :total, :] = jnp.where(low_half, scaled, jnp.zeros_like(scaled))
             gm_s[pair, total:, :] = jnp.where(low_half, jnp.zeros_like(scaled), scaled)
 
@@ -551,7 +553,7 @@
         pair, half = divmod(head, 2)
         rows = slice(head * head_dim, (head + 1) * head_dim)
         row_dot = jnp.sum(
-            gctx_s[rows, :].astype(F32) * ctx_s[rows, :].astype(F32), axis=0, keepdims=True
+            gmt_s[rows, :].astype(F32) * mixed_s[rows, :], axis=0, keepdims=True
         ) * recip_s[head : head + 1, :]
         for at in range(0, total, 128):
             cols = slice(half * total + at, half * total + at + 128)
@@ -810,6 +812,7 @@
             low(3, total, 2 * total),
             low(width, total),
             low(width, total),
+            full(width, total),
             low(width, total),
             full(16, total),
             low(total, width),

time: 67.5 us -> 67.4 us (level)
  no operation moved by 1% of the time
where the time goes in v7:
time: 67.4 us; the launch traced here: 67.2 us
  Pallas kernels  66.6 us (99%)
    pallas_call x1, Pallas kernels, run_layer(): pl.pallas_call(functools.partial(layer_kernel, plane, line, streams, imag...  63.8 us
    pallas_call x1, Pallas kernels, run_layer(): pl.pallas_call(write_kernel, out_shape=tuple((jax.ShapeDtypeStruct(item.s...  2.78 us

profile of v7, /device:TPU:0, one launch (start us, length us, event | category | flops | bytes accessed | tf_op | source)
XLA Modules:
  0.0 67.2 jit_solution(14487235942896219690)
XLA Ops:
  0.6 63.8 %shard_map.218 = (bf16[198,4,768]{2,1,0:T(4,128)(2,1)S(1)}, bf16[50,4,768]{2,1,0:T(4,128)(2,1)S(1)}, f32[198,4,768]{2,1,0:T(4,128)S(1)}, f32[50,768]{1,0:T(8,128)S(1)}, f32[1,1]{1,0:T(1,128)}) custom-call(f32[50,768]{1,0:T(8,128)} %prompts_hbm.1, s32[4,196]{1,0:T(4,128)} %keep_hbm.1, s32[4]{0:T(128)} %counts_hbm.1, f32[768]{0:T(1024)} %ln1_gain_hbm.1, ...), custom_call_target="tpu_custom_call" | custom-call | tf_op jit(solution)/shard_map/pallas_call | solution.py:753
  64.5 2.8 %shard_map.219 = (bf16[198,4,768]{2,1,0:T(4,128)(2,1)}, bf16[50,4,768]{2,1,0:T(4,128)(2,1)}, f32[198,4,768]{2,1,0:T(4,128)}, f32[50,768]{1,0:T(8,128)}, f32[1,1]{1,0:T(1,128)}) custom-call(bf16[198,4,768]{2,1,0:T(4,128)(2,1)S(1)} %get-tuple-element.15.refs_0_, bf16[50,4,768]{2,1,0:T(4,128)(2,1)S(1)} %get-tuple-element.16.refs_1_, ...), custom_call_target="tpu_custom_call" | custom-call | tf_op jit(solution)/shard_map/pallas_call | solution.py:865

commit v8 on v7

--- a/solution.py
+++ b/solution.py
@@ -466,7 +466,7 @@
             before = mid_s[image] if tile.start else rows_s[now2] + out_bias_ref[...][None, :]
             mid_s[image] = before + dot(ctx_s[tile, :].T, w_out[tile, :])
 
-    before, after = 3, 3
+    before, after = 3, 4
     waiting = [head_scores(head) for head in range(before)]
     for head in range(HEADS + after):
         if head + before < HEADS:
@@ -816,7 +816,7 @@
             low(width, total),
             full(16, total),
             low(total, width),
-            full(4, total, 256),
+            full(6, total, 256),
             low(images, total, hidden),
             low(total, hidden),
             full(images, total, width),

time: 67.4 us -> 68.7 us (1.019)
  Pallas kernels: 66.6 us -> 67.9 us
    pallas_call x1, Pallas kernels: 63.8 us -> 65.1 us  [run_layer(): pl.pallas_call(functools.partial(layer_kernel, plane, line, streams, imag...]
where the time goes in v8:
time: 68.7 us; the launch traced here: 68.5 us
  Pallas kernels  67.9 us (99%)
    pallas_call x1, Pallas kernels, run_layer(): pl.pallas_call(functools.partial(layer_kernel, plane, line, streams, imag...  65.1 us
    pallas_call x1, Pallas kernels, run_layer(): pl.pallas_call(write_kernel, out_shape=tuple((jax.ShapeDtypeStruct(item.s...  2.78 us

profile of v8, /device:TPU:0, one launch (start us, length us, event | category | flops | bytes accessed | tf_op | source)
XLA Modules:
  0.0 68.5 jit_solution(12827532883802381406)
XLA Ops:
  0.6 65.1 %shard_map.218 = (bf16[198,4,768]{2,1,0:T(4,128)(2,1)S(1)}, bf16[50,4,768]{2,1,0:T(4,128)(2,1)S(1)}, f32[198,4,768]{2,1,0:T(4,128)S(1)}, f32[50,768]{1,0:T(8,128)S(1)}, f32[1,1]{1,0:T(1,128)}) custom-call(f32[50,768]{1,0:T(8,128)} %prompts_hbm.1, s32[4,196]{1,0:T(4,128)} %keep_hbm.1, s32[4]{0:T(128)} %counts_hbm.1, f32[768]{0:T(1024)} %ln1_gain_hbm.1, ...), custom_call_target="tpu_custom_call" | custom-call | tf_op jit(solution)/shard_map/pallas_call | solution.py:753
  65.7 2.8 %shard_map.219 = (bf16[198,4,768]{2,1,0:T(4,128)(2,1)}, bf16[50,4,768]{2,1,0:T(4,128)(2,1)}, f32[198,4,768]{2,1,0:T(4,128)}, f32[50,768]{1,0:T(8,128)}, f32[1,1]{1,0:T(1,128)}) custom-call(bf16[198,4,768]{2,1,0:T(4,128)(2,1)S(1)} %get-tuple-element.15.refs_0_, bf16[50,4,768]{2,1,0:T(4,128)(2,1)S(1)} %get-tuple-element.16.refs_1_, ...), custom_call_target="tpu_custom_call" | custom-call | tf_op jit(solution)/shard_map/pallas_call | solution.py:865
